TPU v7x, 512 devices: a whole 4x4x16 slice. The times are simulated.
512 devices in a mesh: pipe: 16 (over z), ctx: 32 (over y, x, core).
Axes of the slice: x: 4, y: 4, z: 16, core: 2. Of those that a mesh axis runs over, the one named last changes fastest.
Arguments:
- queries: bfloat16 [16, 4096, 1024], P('pipe', 'ctx'), may hold values from -80 to 80
- keys: bfloat16 [16, 4096, 128], P('pipe', 'ctx'), may hold values from -4 to 4
- values: bfloat16 [16, 4096, 128], P('pipe', 'ctx'), may hold values from -6 to 6
- attn_out: bfloat16 [16, 4096, 1024], P('pipe', 'ctx'), may hold values from -6 to 6
- grad_out: bfloat16 [16, 4096, 1024], P('pipe', 'ctx'), may hold values from -6 to 6
- doc_lengths: int32 [16], replicated, may hold values from 1 to 1024, 4096 in all
- pair_of_rank: int32 [32], replicated, may hold values from 0 to 31, each once
Outputs:
- query_grad: bfloat16 [16, 4096, 1024], P('pipe', 'ctx')
- handed_grad: bfloat16 [16, 4096, 1024], P('pipe', 'ctx')
- key_grad: bfloat16 [16, 4096, 128], P('pipe', 'ctx')
- value_grad: bfloat16 [16, 4096, 128], P('pipe', 'ctx')
Inputs may be any that keep to these rules, and one draw needn't show every extreme that they name: `doc_lengths`: the lengths of the 16 documents packed in order into the 4096 positions; they sum to 4096, the same documents for every section. `pair_of_rank`: each stretch pair appears once; pair p is the stretches of positions p * 64 to (p + 1) * 64 - 1 and (63 - p) * 64 onwards.
All inputs are finite; a program needn't handle non-finite values.
Results may differ from a plain program's by a relative error of at most 0.015.
Values may be sent and summed in bfloat16 or wider, within the bound.
A program may use at most 64 MiB of HBM per device.

v0:
```python
import math

import jax
import jax.numpy as jnp
from jax import lax
from jax.sharding import PartitionSpec as P

HQ = 8
HD = 128


NEG = -1e30


def shifted(x, axis, by):
    count = lax.axis_size(axis)
    return lax.ppermute(x, axis, [(i, (i + by) % count) for i in range(count)])


def row_positions(rows, pair_table, stretch):
    count = pair_table.shape[0]
    ranks = rows // (2 * stretch)
    within = rows % (2 * stretch)
    match = ranks[:, None] == jnp.arange(count, dtype=jnp.int32)[None, :]
    pairs = jnp.sum(jnp.where(match, pair_table[None, :], 0), axis=1)
    early = pairs * stretch + within
    late = (2 * count - 1 - pairs) * stretch + within - stretch
    return jnp.where(within < stretch, early, late)


def doc_numbers(positions, doc_lengths):
    ends = jnp.cumsum(doc_lengths)
    return jnp.sum((positions[:, None] >= ends[None, :]).astype(jnp.int32), axis=1)


def block_scores(query_heads, key_block, scale):
    return (
        jnp.einsum("qhd,kd->hqk", query_heads, key_block, preferred_element_type=jnp.float32)
        * scale
    )


def block_stats(carry, query_heads, key_block, allowed, scale):
    top, total = carry
    scores = jnp.where(allowed[None], block_scores(query_heads, key_block, scale), NEG)
    new_top = jnp.maximum(top, jnp.max(scores, axis=2))
    weights = jnp.where(allowed[None], jnp.exp(scores - new_top[:, :, None]), 0.0)
    return (new_top, total * jnp.exp(top - new_top) + jnp.sum(weights, axis=2))


def block_grads(query_heads, grad_heads, delta, lse, key_block, value_block, allowed, scale):
    scores = block_scores(query_heads, key_block, scale)
    probs = jnp.where(allowed[None], jnp.exp(scores - lse[:, :, None]), 0.0)
    probs_low = probs.astype(jnp.bfloat16)
    dprobs = jnp.einsum("qhd,kd->hqk", grad_heads, value_block, preferred_element_type=jnp.float32)
    dscores = (probs * (dprobs - delta[:, :, None])).astype(jnp.bfloat16)
    dquery = jnp.einsum("hqk,kd->qhd", dscores, key_block, preferred_element_type=jnp.float32)
    dkey = (
        jnp.einsum("hqk,qhd->kd", dscores, query_heads, preferred_element_type=jnp.float32) * scale
    )
    dvalue = jnp.einsum("hqk,qhd->kd", probs_low, grad_heads, preferred_element_type=jnp.float32)
    return (dquery, dkey, dvalue)


def on_device(queries, keys, values, attn_out, grad_out, doc_lengths, pair_of_rank):
    tok = queries.shape[1]
    stretch = tok // 2
    ranks = lax.axis_size("ctx")
    seq_len = tok * ranks
    scale = 1.0 / math.sqrt(HD)
    query_heads = queries[0].reshape(tok, HQ, HD)
    grad_heads = grad_out[0].reshape(tok, HQ, HD)
    out_heads = attn_out[0].reshape(tok, HQ, HD)
    key_local = keys[0]
    value_local = values[0]
    me = lax.axis_index("ctx")
    own_rows = me * tok + jnp.arange(tok, dtype=jnp.int32)
    own_pos = row_positions(own_rows, pair_of_rank, stretch)
    own_doc = doc_numbers(own_pos, doc_lengths)
    delta = jnp.einsum("qhd,qhd->hq", grad_heads, out_heads, preferred_element_type=jnp.float32)

    def allowed_for(rows):
        positions = row_positions(rows, pair_of_rank, stretch)
        documents = doc_numbers(positions, doc_lengths)
        return (own_doc[:, None] == documents[None, :]) & (positions[None, :] <= own_pos[:, None])

    start_top = jnp.full((HQ, tok), NEG, jnp.float32)
    start_total = jnp.zeros((HQ, tok), jnp.float32)
    dquery_zero = jnp.zeros((tok, HQ, HD), jnp.float32)
    gathered_keys, gathered_values = (
        lax.all_gather(key_local, "ctx", axis=0, tiled=True),
        lax.all_gather(value_local, "ctx", axis=0, tiled=True),
    )
    width = math.gcd(seq_len, 512)
    count = seq_len // width

    def stats_step(index, carry):
        start = index * width
        key_block = lax.dynamic_slice_in_dim(gathered_keys, start, width, 0)
        allowed = allowed_for(start + jnp.arange(width, dtype=jnp.int32))
        return block_stats(carry, query_heads, key_block, allowed, scale)

    top, total = lax.fori_loop(0, count, stats_step, (start_top, start_total))
    lse = top + jnp.log(total)

    def grad_step(index, carry):
        start = index * width
        key_block = lax.dynamic_slice_in_dim(gathered_keys, start, width, 0)
        value_block = lax.dynamic_slice_in_dim(gathered_values, start, width, 0)
        allowed = allowed_for(start + jnp.arange(width, dtype=jnp.int32))
        dquery_sum, key_terms, value_terms = carry
        dquery, dkey, dvalue = block_grads(
            query_heads, grad_heads, delta, lse, key_block, value_block, allowed, scale
        )
        key_terms = lax.dynamic_update_slice_in_dim(key_terms, dkey, start, 0)
        value_terms = lax.dynamic_update_slice_in_dim(value_terms, dvalue, start, 0)
        return (dquery_sum + dquery, key_terms, value_terms)

    empty_terms = jnp.zeros((seq_len, HD), jnp.float32)
    dquery_sum, key_terms, value_terms = lax.fori_loop(
        0, count, grad_step, (dquery_zero, empty_terms, empty_terms)
    )
    key_sum, value_sum = (
        lax.psum_scatter(
            key_terms.astype(jnp.bfloat16), "ctx", scatter_dimension=0, tiled=True
        ).astype(jnp.float32),
        lax.psum_scatter(
            value_terms.astype(jnp.bfloat16), "ctx", scatter_dimension=0, tiled=True
        ).astype(jnp.float32),
    )
    query_grad = (dquery_sum * scale).reshape(tok, HQ * HD).astype(jnp.bfloat16)[None]
    handed_grad = shifted(query_grad, "pipe", -1)
    key_grad = key_sum.astype(jnp.bfloat16)[None]
    value_grad = value_sum.astype(jnp.bfloat16)[None]
    return (query_grad, handed_grad, key_grad, value_grad)


def solution(mesh):
    placed = (
        P("pipe", "ctx", None),
        P("pipe", "ctx", None),
        P("pipe", "ctx", None),
        P("pipe", "ctx", None),
        P("pipe", "ctx", None),
        P(),
        P(),
    )
    return jax.shard_map(
        on_device,
        mesh=mesh,
        in_specs=placed,
        out_specs=(
            P("pipe", "ctx", None),
            P("pipe", "ctx", None),
            P("pipe", "ctx", None),
            P("pipe", "ctx", None),
        ),
        check_vma=False,
    )
```

profile of v0, /device:TPU:6, one launch (start us, length us, event | category | flops | bytes accessed | tf_op | source)
XLA Modules:
  0.0 418.6 jit_solution(8731508337626048972)
XLA Ops:
  14.3 58.8 %all-gather.5.cloned.1.call-done = bf16[1,4096,128]{2,1,0:T(8,128)(2,1)} async-done(((bf16[1,128,128]{2,1,0:T(8,128)(2,1)}), bf16[1,4096,128]{2,1,0:T(8,128)(2,1)}) %all-gather.5.cloned.1.call-update) | async-done | bytes 1048592 | tf_op jit(solution)/shard_map/all_gather | solution.py:91
  73.1 20.0 %while.38 = (s32[]{:T(128)}, f32[8,128]{1,0:T(8,128)S(1)}, f32[8,128]{1,0:T(8,128)S(1)}, s32[128]{0:T(128)S(1)}, s32[32]{0:T(128)S(1)}, /*index=5*/s32[1,16]{1,0...) while((s32[]{:T(128)}, f32[8,128]{1,0:T(8,128)S(1)}, ...), condition=%wide.region_8.9_spmd.clone, body=%wide.region_3.8_spmd.clone.sunk | while | flops 138704896 | bytes 4857218 | solution.py:103
  73.5 1.5 fusion.56
  76.0 1.5 fusion.56
  78.5 1.5 fusion.56
  81.0 1.5 fusion.56
  83.5 1.5 fusion.56
  86.0 1.5 fusion.56
  88.5 1.5 fusion.56
  91.0 1.5 fusion.56
  93.1 40.5 %all-gather.7.cloned.1.call-done = bf16[1,4096,128]{2,1,0:T(8,128)(2,1)} async-done(((bf16[1,128,128]{2,1,0:T(8,128)(2,1)}), bf16[1,4096,128]{2,1,0:T(8,128)(2,1)}) %all-gather.7.cloned.1.call-update) | async-done | bytes 1048592 | tf_op jit(solution)/shard_map/all_gather | solution.py:92
  135.8 69.8 %while.39 = (s32[]{:T(128)}, f32[128,8,128]{0,2,1:T(8,128)}, bf16[4096,128]{1,0:T(8,128)(2,1)}, bf16[4096,128]{1,0:T(8,128)(2,1)}, bf16[4096,128]{1,0:T(8,128)(2...) while((s32[]{:T(128)}, f32[128,8,128]{0,2,1:T(8,128)}, ...), condition=%wide.region_12.13_spmd.clone, body=%wide.region_9.12_spmd.clone.sunk | while | flops 675374080 | bytes 12611001 | solution.py:120
  136.3 1.6 fusion.68
  137.9 1.3 fusion.69
  139.2 2.0 fusion.71
  141.3 2.0 fusion.70
  144.8 1.6 fusion.68
  146.4 1.3 fusion.69
  147.8 2.0 fusion.71
  149.8 2.2 fusion.70
  153.6 1.6 fusion.68
  155.2 1.3 fusion.69
  156.5 2.0 fusion.71
  158.5 2.2 fusion.70
  162.3 1.6 fusion.68
  163.9 1.3 fusion.69
  165.3 2.0 fusion.71
  167.3 2.2 fusion.70
  171.1 1.6 fusion.68
  172.7 1.3 fusion.69
  174.0 2.0 fusion.71
  176.1 2.2 fusion.70
  179.8 1.6 fusion.68
  181.4 1.3 fusion.69
  182.7 2.1 fusion.71
  184.8 2.2 fusion.70
  188.6 1.6 fusion.68
  190.2 1.3 fusion.69
  191.5 2.0 fusion.71
  193.5 2.2 fusion.70
  197.3 1.6 fusion.68
  198.9 1.3 fusion.69
  200.2 2.0 fusion.71
  202.3 2.2 fusion.70
  206.9 6.0 %collective-permute-start = (bf16[1,128,1024]{2,1,0:T(8,128)(2,1)S(1)}, bf16[1,128,1024]{2,1,0:T(8,128)(2,1)S(1)}, u32[]{:S(2)}, u32[]{:S(2)}) collective-permute-start(bf16[1,128,1024]{2,1,0:T(8,128)(2,1)S(1)} %copy.40), channel_id=1, source_target_pairs={{0,480},{32,0},{64,32},{96,64},{128,96},{160,128},{192,160},{224,1... | collective-permute-start | bytes 786440 | tf_op jit(solution)/shard_map/ppermute | solution.py:17
  212.9 5.9 %collective-permute-done = bf16[1,128,1024]{2,1,0:T(8,128)(2,1)S(1)} collective-permute-done((bf16[1,128,1024]{2,1,0:T(8,128)(2,1)S(1)}, bf16[1,128,1024]{2,1,0:T(8,128)(2,1)S(1)}, u32[]{:S(2)}, u32[]{:S(2)}) %collective-permute-start) | collective-permute-done | bytes 262176 | tf_op jit(solution)/shard_map/ppermute | solution.py:17
  218.8 87.4 %reduce-scatter.3.cloned.1.call-done = bf16[128,128]{1,0:T(8,128)(2,1)} async-done(((bf16[4096,128]{1,0:T(8,128)(2,1)}), bf16[128,128]{1,0:T(8,128)(2,1)}) %reduce-scatter.3.cloned.1.call-update) | async-done | bytes 32784 | tf_op jit(solution)/shard_map/reduce_scatter | solution.py:124
  306.2 105.2 %reduce-scatter.5.cloned.1.call-done = bf16[128,128]{1,0:T(8,128)(2,1)} async-done(((bf16[4096,128]{1,0:T(8,128)(2,1)}), bf16[128,128]{1,0:T(8,128)(2,1)}) %reduce-scatter.5.cloned.1.call-update) | async-done | bytes 32784 | tf_op jit(solution)/shard_map/reduce_scatter | solution.py:127
  (158 shorter events, 30.8 us)
Async XLA Ops:
  7.2 6.5 %copy-start.1 = (bf16[1,128,1024]{2,1,0:T(8,128)(2,1)S(1)}, bf16[1,128,1024]{2,1,0:T(8,128)(2,1)}, u32[]{:S(2)}) copy-start(bf16[1,128,1024]{2,1,0:T(8,128)(2,1)} %param.14) | copy-start | bytes 786436
  7.2 65.9 %all-gather.5.cloned.1.call-start = ((), (), s32[]{:S(2)}) async-start(), calls=%async_computation.4 | async-start | bytes 1081344 | tf_op jit(solution)/shard_map/all_gather | solution.py:91
  7.9 125.7 %all-gather.7.cloned.1.call-start = ((), (), s32[]{:S(2)}) async-start(), calls=%async_computation.5 | async-start | bytes 1081344 | tf_op jit(solution)/shard_map/all_gather | solution.py:92
  8.7 297.5 %reduce-scatter.3.cloned.1.call-start = ((), (), s32[]{:S(2)}) async-start(), calls=%async_computation.2 | async-start | bytes 1081344 | tf_op jit(solution)/shard_map/reduce_scatter | solution.py:124
  10.4 62.8 %copy-start.3 = (s32[32]{0:T(128)S(1)}, s32[32]{0:T(128)}, u32[]{:S(2)}) copy-start(s32[32]{0:T(128)} %param.17) | copy-start | bytes 388
  205.6 1.0 copy-start
  205.7 205.7 %reduce-scatter.5.cloned.1.call-start = ((), (), s32[]{:S(2)}) async-start(), calls=%async_computation.3 | async-start | bytes 1081344 | tf_op jit(solution)/shard_map/reduce_scatter | solution.py:127
  206.9 205.2 %copy-start.2 = (bf16[1,128,1024]{2,1,0:T(8,128)(2,1)}, bf16[1,128,1024]{2,1,0:T(8,128)(2,1)S(1)}, u32[]{:S(2)}) copy-start(bf16[1,128,1024]{2,1,0:T(8,128)(2,1)S(1)} %copy.40) | copy-start | bytes 786436
  206.9 11.9 %collective-permute-start = (bf16[1,128,1024]{2,1,0:T(8,128)(2,1)S(1)}, bf16[1,128,1024]{2,1,0:T(8,128)(2,1)S(1)}, u32[]{:S(2)}, u32[]{:S(2)}) collective-permute-start(bf16[1,128,1024]{2,1,0:T(8,128)(2,1)S(1)} %copy.40), channel_id=1, source_target_pairs={{0,480},{32,0},{64,32},{96,64},{128,96},{160,128},{192,160},{224,1... | collective-permute-start | bytes 786440 | tf_op jit(solution)/shard_map/ppermute | solution.py:17
Sparse Core Ops, SparseCore 0:
  11.1 61.9 all-gather.4
  76.2 57.3 all-gather.6
  205.8 100.3 reduce-scatter.2
  311.0 100.3 reduce-scatter.4
where the time goes:
time: 420 us; the launch traced here: 419 us
  waiting for transfers between devices  300 us (71%)
  matrix products  78 us (19%)
  between operations  13.9 us (3%)
  other arithmetic  12.8 us (3%)
  local copies, waits for them, and re-layouts  7.16 us (2%)
  starting transfers between devices  6.12 us (1%)
    reduce_scatter x1, waiting for transfers between devices, on_device(): lax.psum_scatter(value_terms.astype(jnp.bfloat16), 'ctx', scatter_dimensi...  105 us
    reduce_scatter x1, waiting for transfers between devices, on_device(): lax.psum_scatter(key_terms.astype(jnp.bfloat16), 'ctx', scatter_dimension...  87.4 us
    all_gather x1, waiting for transfers between devices, on_device(): lax.all_gather(key_local, 'ctx', axis=0, tiled=True)  58.8 us
    all_gather x1, waiting for transfers between devices, on_device(): lax.all_gather(value_local, 'ctx', axis=0, tiled=True)  40.5 us
    dot_general x16, matrix products, block_scores(): jnp.einsum('qhd,kd->hqk', query_heads, key_block, preferred_element_type=...  24.5 us
    dot_general x8, matrix products, block_grads(): jnp.einsum('hqk,kd->qhd', dscores, key_block, preferred_element_type=jnp....  17.7 us
    dot_general x8, matrix products, block_grads(): jnp.einsum('hqk,qhd->kd', dscores, query_heads, preferred_element_type=jn...  16.3 us
    dot_general x8, matrix products, block_grads(): jnp.einsum('qhd,kd->hqk', grad_heads, value_block, preferred_element_type...  10.8 us
  transfers between devices with their start and end apart: 5, of which 5 were waited for; matrix products, arithmetic and copies ran while one was open for 6% of the time, Pallas kernels for 0%

commit v1 on v0

v1 whole, which is shorter than its diff:
```python
import math

import jax
import jax.numpy as jnp
from jax import lax
from jax.experimental import pallas as pl
from jax.experimental.pallas import tpu as pltpu
from jax.sharding import PartitionSpec as P

HQ = 8
HD = 128
ST = 64
RANKS = 32
SIDE = 4
STRETCHES = 2 * RANKS
WIN = 18
CHUNK = 384
CHUNKS = WIN * ST // CHUNK
ROWS = HQ * ST
GROUP = 2 * SIDE
NEG = -1e30
MESH = pl.DeviceIdType.MESH
F32 = jnp.float32
BF16 = jnp.bfloat16


class Place:
    def __init__(self):
        me = lax.axis_index("ctx")
        self.core = lax.rem(me, 2)
        chip = me // 2
        self.x = lax.rem(chip, SIDE)
        self.y = chip // SIDE

    def at(self, dx, dy):
        x = lax.rem(self.x + dx + SIDE, SIDE)
        y = lax.rem(self.y + dy + SIDE, SIDE)
        return (y * SIDE + x) * 2 + self.core

    def sibling(self):
        return (self.y * SIDE + self.x) * 2 + 1 - self.core

    def neighbours(self):
        return [self.sibling(), self.at(1, 0), self.at(-1, 0), self.at(0, 1), self.at(0, -1)]

    def order(self, fast_is_x):
        if fast_is_x:
            return self.x, self.y, (lambda d: self.at(d, 0)), (lambda d: self.at(0, d))
        return self.y, self.x, (lambda d: self.at(0, d)), (lambda d: self.at(d, 0))


def step(i, d):
    return lax.rem(i + d + SIDE, SIDE)


def in_turn(*streams):
    live = list(streams)
    while live:
        for stream in list(live):
            if next(stream, StopIteration) is StopIteration:
                live.remove(stream)


def sender(send_sem, recv_sem):
    sent = {}

    def send(i, src, dst, device):
        copy = pltpu.make_async_remote_copy(
            src_ref=src, dst_ref=dst, send_sem=send_sem.at[i], recv_sem=recv_sem.at[i],
            device_id={"ctx": device}, device_id_type=MESH,
        )
        copy.start()
        sent[i] = copy

    return sent, send


def gather_stream(place, fast_is_x, own, full, own_sem, send_sem, recv_sem):
    fast, slow, along_fast, along_slow = place.order(fast_is_x)
    sent, send = sender(send_sem, recv_sem)
    half = place.core * (SIDE * GROUP)

    def block(d, lo=0, n=2):
        return full.at[pl.ds(half + slow * GROUP + step(fast, d) * 2 + lo, n)]

    def group(d, lo=0, n=GROUP):
        return full.at[pl.ds(half + step(slow, d) * GROUP + lo, n)]

    send(0, own, block(0), along_fast(1))
    send(1, own, block(0), along_fast(-1))
    mine = pltpu.make_async_copy(own, block(0), own_sem)
    mine.start()
    yield
    sent[0].wait_recv()
    send(2, block(-1, 0, 1), block(-1, 0, 1), along_fast(1))
    yield
    sent[1].wait_recv()
    send(3, block(1, 1, 1), block(1, 1, 1), along_fast(-1))
    mine.wait()
    yield
    sent[2].wait_recv()
    sent[3].wait_recv()
    send(4, group(0), group(0), along_slow(1))
    send(5, group(0), group(0), along_slow(-1))
    send(6, group(0), group(0), place.sibling())
    yield
    sent[4].wait_recv()
    send(7, group(-1, 0, SIDE), group(-1, 0, SIDE), along_slow(1))
    send(9, group(-1), group(-1), place.sibling())
    yield
    sent[5].wait_recv()
    send(8, group(1, SIDE, SIDE), group(1, SIDE, SIDE), along_slow(-1))
    send(10, group(1), group(1), place.sibling())
    yield
    sent[7].wait_recv()
    sent[8].wait_recv()
    send(11, group(2), group(2), place.sibling())
    yield
    for i in (6, 9, 10, 11):
        sent[i].wait_recv()
    for i in range(12):
        sent[i].wait_send()


def gather_kernel(k_ref, v_ref, gk_ref, gv_ref, own_sem, k_send, k_recv, v_send, v_recv):
    place = Place()
    barrier = pltpu.get_barrier_semaphore()
    for device in place.neighbours():
        pl.semaphore_signal(barrier, inc=1, device_id={"ctx": device}, device_id_type=MESH)
    pl.semaphore_wait(barrier, 5)
    in_turn(
        gather_stream(place, True, k_ref, gk_ref, own_sem.at[0], k_send, k_recv),
        gather_stream(place, False, v_ref, gv_ref, own_sem.at[1], v_send, v_recv),
    )


def add(*terms):
    total = terms[0].astype(F32)
    for term in terms[1:]:
        total = total + term.astype(F32)
    return total.astype(BF16)


def scatter_stream(place, fast_is_x, part, out, bufs, send_sem, recv_sem):
    sib, acc, across_a, across_b, from_low, from_high, line, near_a, near_b, end_low, end_high = bufs
    fast, slow, along_fast, along_slow = place.order(fast_is_x)
    sent, send = sender(send_sem, recv_sem)
    mine, other = place.core * (SIDE * GROUP), (1 - place.core) * (SIDE * GROUP)

    def at(d, lo=0, n=GROUP):
        return pl.ds(step(slow, d) * GROUP + lo, n)

    def merge(d):
        acc[at(d)] = add(part[pl.ds(mine + step(slow, d) * GROUP, GROUP)], sib[at(d)])

    for i, d in enumerate((2, 1, -1, 0)):
        send(i, part.at[pl.ds(other + step(slow, d) * GROUP, GROUP)], sib.at[at(d)], place.sibling())
    yield
    sent[0].wait_recv()
    merge(2)
    send(4, acc.at[at(2, 0, SIDE)], across_a, along_slow(1))
    send(5, acc.at[at(2, SIDE, SIDE)], across_b, along_slow(-1))
    yield
    sent[1].wait_recv()
    merge(1)
    send(6, acc.at[at(1, SIDE, SIDE)], from_low.at[pl.ds(SIDE, SIDE)], along_slow(1))
    yield
    sent[2].wait_recv()
    merge(-1)
    send(7, acc.at[at(-1, 0, SIDE)], from_high.at[pl.ds(0, SIDE)], along_slow(-1))
    yield
    sent[3].wait_recv()
    merge(0)
    yield
    sent[4].wait_recv()
    acc[at(1, 0, SIDE)] = add(acc[at(1, 0, SIDE)], across_a[...])
    send(8, acc.at[at(1, 0, SIDE)], from_low.at[pl.ds(0, SIDE)], along_slow(1))
    yield
    sent[5].wait_recv()
    acc[at(-1, SIDE, SIDE)] = add(acc[at(-1, SIDE, SIDE)], across_b[...])
    send(9, acc.at[at(-1, SIDE, SIDE)], from_high.at[pl.ds(SIDE, SIDE)], along_slow(-1))
    yield
    for i in (6, 7, 8, 9):
        sent[i].wait_recv()
    line[...] = add(acc[at(0)], from_low[...], from_high[...])

    def one(d, lo, n=1):
        return pl.ds(step(fast, d) * 2 + lo, n)

    send(10, line.at[one(2, 0)], near_a, along_fast(1))
    send(11, line.at[one(2, 1)], near_b, along_fast(-1))
    send(12, line.at[one(1, 1)], end_low.at[pl.ds(1, 1)], along_fast(1))
    send(13, line.at[one(-1, 0)], end_high.at[pl.ds(0, 1)], along_fast(-1))
    yield
    sent[10].wait_recv()
    line[one(1, 0)] = add(line[one(1, 0)], near_a[...])
    send(14, line.at[one(1, 0)], end_low.at[pl.ds(0, 1)], along_fast(1))
    yield
    sent[11].wait_recv()
    line[one(-1, 1)] = add(line[one(-1, 1)], near_b[...])
    send(15, line.at[one(-1, 1)], end_high.at[pl.ds(1, 1)], along_fast(-1))
    yield
    for i in (12, 13, 14, 15):
        sent[i].wait_recv()
    out[...] = add(line[one(0, 0, 2)], end_low[...], end_high[...])
    for i in range(16):
        sent[i].wait_send()


SCATTER_BUFS = (SIDE * GROUP, SIDE * GROUP, SIDE, SIDE, GROUP, GROUP, GROUP, 1, 1, 2, 2)


def scatter_kernel(kp_ref, vp_ref, dq_ref, kg_ref, vg_ref, handed_ref, *scratch):
    count = len(SCATTER_BUFS)
    k_bufs, v_bufs = scratch[:count], scratch[count : 2 * count]
    k_send, k_recv, v_send, v_recv, hand_sem = scratch[2 * count :]
    place = Place()
    section, sections = lax.axis_index("pipe"), lax.axis_size("pipe")
    below = lax.rem(section + sections - 1, sections)
    above = lax.rem(section + 1, sections)
    barrier = pltpu.get_barrier_semaphore()
    for device in place.neighbours():
        pl.semaphore_signal(barrier, inc=1, device_id={"ctx": device}, device_id_type=MESH)
    for device in (below, above):
        pl.semaphore_signal(barrier, inc=1, device_id={"pipe": device}, device_id_type=MESH)
    pl.semaphore_wait(barrier, 7)
    hand = pltpu.make_async_remote_copy(
        src_ref=dq_ref, dst_ref=handed_ref, send_sem=hand_sem.at[0], recv_sem=hand_sem.at[1],
        device_id={"pipe": below}, device_id_type=MESH,
    )
    hand.start()
    in_turn(
        scatter_stream(place, True, kp_ref, kg_ref, k_bufs, k_send, k_recv),
        scatter_stream(place, False, vp_ref, vg_ref, v_bufs, v_send, v_recv),
    )
    hand.wait()


def dot(a, b, over):
    return lax.dot_general(a, b, ((over[:1], over[1:]), ((), ())), preferred_element_type=F32)


def attend_kernel(
    docs, pairs, q_ref, o_ref, g_ref, k_ref, v_ref, dq_ref, kp_ref, vp_ref,
    rank_of_pair, q_rows, g_rows, key_win, value_win, work, key_terms, value_terms,
):
    scale = 1.0 / math.sqrt(HD)
    pair = pairs[lax.axis_index("ctx")]

    def note(r, carry):
        rank_of_pair[pairs[r]] = r
        return carry

    lax.fori_loop(0, RANKS, note, 0)

    def places(t):
        late = (t >= RANKS).astype(jnp.int32)
        rank = rank_of_pair[jnp.where(t >= RANKS, STRETCHES - 1 - t, t)]
        core, chip = lax.rem(rank, 2), rank // 2
        turned = lax.rem(chip, SIDE) * SIDE + chip // SIDE
        size = SIDE * SIDE
        return (core * size + chip) * 2 + late, (core * size + turned) * 2 + late

    kp_ref[...] = jnp.zeros_like(kp_ref)
    vp_ref[...] = jnp.zeros_like(vp_ref)
    bases = (pair, STRETCHES - 1 - pair)
    lane = lax.rem(lax.broadcasted_iota(jnp.int32, (1, ROWS), 1), ST)
    for which in range(2):
        base = bases[which]
        lowest = (base - (WIN - 1)) * ST
        rows = slice(which * ST, (which + 1) * ST)
        for h in range(HQ):
            q_rows[h * ST : (h + 1) * ST] = q_ref[rows, h * HD : (h + 1) * HD]
            g_rows[h * ST : (h + 1) * ST] = g_ref[rows, h * HD : (h + 1) * HD]
        products = jnp.concatenate(
            [
                g_ref[rows, h * HD : (h + 1) * HD].astype(F32) * o_ref[rows, h * HD : (h + 1) * HD].astype(F32)
                for h in range(HQ)
            ],
            axis=0,
        )
        delta = jnp.sum(jnp.transpose(products), axis=0, keepdims=True)
        for j in range(WIN):
            k_at, v_at = places(jnp.maximum(base - (WIN - 1) + j, 0))
            key_win[j * ST : (j + 1) * ST] = k_ref[k_at]
            value_win[j * ST : (j + 1) * ST] = v_ref[v_at]
        position = base * ST + lane
        start, first, end = jnp.zeros_like(position), jnp.int32(0), jnp.int32(0)
        for d in range(docs.shape[0]):
            end = end + docs[d]
            start = jnp.where(position >= end, end, start)
            first = jnp.where(base * ST >= end, end, first)
        low, high = start - lowest, position - lowest
        begin = (first - lowest) // CHUNK

        def scores(c, top):
            at = pl.multiple_of(c * CHUNK, CHUNK)
            found = dot(key_win[pl.ds(at, CHUNK)], q_rows[...], (1, 1))
            where = lax.broadcasted_iota(jnp.int32, (CHUNK, ROWS), 0) + at
            found = jnp.where((where >= low) & (where <= high), found, NEG)
            work[c] = found
            return jnp.maximum(top, jnp.max(found, axis=0, keepdims=True))

        top = lax.fori_loop(begin, CHUNKS, scores, jnp.full((1, ROWS), NEG, F32))

        def weigh(c, total):
            weights = jnp.exp2((work[c] - top) * (scale * math.log2(math.e)))
            work[c] = weights
            return total + jnp.sum(weights, axis=0, keepdims=True)

        total = lax.fori_loop(begin, CHUNKS, weigh, jnp.zeros((1, ROWS), F32))
        inverse = 1.0 / total

        def grads(c, dq_sum):
            at = pl.multiple_of(c * CHUNK, CHUNK)
            probs = work[c] * inverse
            value_terms[which, pl.ds(at, CHUNK)] = dot(probs.astype(BF16), g_rows[...], (1, 0))
            dprobs = dot(value_win[pl.ds(at, CHUNK)], g_rows[...], (1, 1))
            dscores = (probs * (dprobs - delta)).astype(BF16)
            key_terms[which, pl.ds(at, CHUNK)] = dot(dscores, q_rows[...], (1, 0)) * scale
            turned = jnp.transpose(key_win[pl.ds(at, CHUNK)])
            return dq_sum + dot(turned, dscores, (1, 0))

        dq_sum = lax.fori_loop(begin, CHUNKS, grads, jnp.zeros((HD, ROWS), F32))
        dq_rows = (jnp.transpose(dq_sum) * scale).astype(BF16)
        for h in range(HQ):
            dq_ref[rows, h * HD : (h + 1) * HD] = dq_rows[h * ST : (h + 1) * ST]

        def clear(c, carry):
            at = pl.multiple_of(c * CHUNK, CHUNK)
            key_terms[which, pl.ds(at, CHUNK)] = jnp.zeros((CHUNK, HD), F32)
            value_terms[which, pl.ds(at, CHUNK)] = jnp.zeros((CHUNK, HD), F32)
            return carry

        lax.fori_loop(0, begin, clear, 0)

    early, late = bases[0] - (WIN - 1), bases[1] - (WIN - 1)

    def put_early(j, carry):
        t = early + j

        @pl.when((t >= 0) & (t < late))
        def _():
            k_at, v_at = places(t)
            at = pl.multiple_of(j * ST, ST)
            kp_ref[k_at] = key_terms[0, pl.ds(at, ST)].astype(BF16)
            vp_ref[v_at] = value_terms[0, pl.ds(at, ST)].astype(BF16)

        return carry

    lax.fori_loop(0, WIN, put_early, 0)

    def put_late(j, carry):
        t = late + j
        k_at, v_at = places(t)
        at = pl.multiple_of(j * ST, ST)
        shared = t - early
        both = (shared >= 0) & (shared < WIN)
        near = pl.multiple_of(jnp.clip(shared, 0, WIN - 1) * ST, ST)
        kp_ref[k_at] = (
            key_terms[1, pl.ds(at, ST)] + jnp.where(both, key_terms[0, pl.ds(near, ST)], 0.0)
        ).astype(BF16)
        vp_ref[v_at] = (
            value_terms[1, pl.ds(at, ST)] + jnp.where(both, value_terms[0, pl.ds(near, ST)], 0.0)
        ).astype(BF16)
        return carry

    lax.fori_loop(0, WIN, put_late, 0)


def on_device(queries, keys, values, attn_out, grad_out, doc_lengths, pair_of_rank):
    vmem = pl.BlockSpec(memory_space=pltpu.VMEM)
    smem = pl.BlockSpec(memory_space=pltpu.SMEM)
    hbm = pl.BlockSpec(memory_space=pl.ANY)
    full = jax.ShapeDtypeStruct((STRETCHES, ST, HD), BF16)
    own = jax.ShapeDtypeStruct((2, ST, HD), BF16)
    tok = 2 * ST
    dma = pltpu.SemaphoreType.DMA
    all_keys, all_values = pl.pallas_call(
        gather_kernel,
        out_shape=(full, full),
        in_specs=[vmem] * 2,
        out_specs=(vmem, vmem),
        scratch_shapes=[dma((2,)), dma((12,)), dma((12,)), dma((12,)), dma((12,))],
        compiler_params=pltpu.CompilerParams(collective_id=0, has_side_effects=True),
        name="gather_keys_values",
    )(keys.reshape(2, ST, HD), values.reshape(2, ST, HD))
    query_grad, key_part, value_part = pl.pallas_call(
        attend_kernel,
        out_shape=(jax.ShapeDtypeStruct((tok, HQ * HD), BF16), full, full),
        in_specs=[smem] * 2 + [vmem] * 5,
        out_specs=(vmem,) * 3,
        scratch_shapes=[
            pltpu.SMEM((RANKS,), jnp.int32),
            pltpu.VMEM((ROWS, HD), BF16),
            pltpu.VMEM((ROWS, HD), BF16),
            pltpu.VMEM((WIN * ST, HD), BF16),
            pltpu.VMEM((WIN * ST, HD), BF16),
            pltpu.VMEM((CHUNKS, CHUNK, ROWS), F32),
            pltpu.VMEM((2, WIN * ST, HD), F32),
            pltpu.VMEM((2, WIN * ST, HD), F32),
        ],
        name="attend_backward",
    )(doc_lengths, pair_of_rank, queries[0], attn_out[0], grad_out[0], all_keys, all_values)
    bufs = [pltpu.VMEM((n, ST, HD), BF16) for n in SCATTER_BUFS]
    key_grad, value_grad, handed = pl.pallas_call(
        scatter_kernel,
        out_shape=(own, own, jax.ShapeDtypeStruct((tok, HQ * HD), BF16)),
        in_specs=[vmem, vmem, hbm],
        out_specs=(vmem, vmem, hbm),
        scratch_shapes=bufs + bufs + [dma((16,)), dma((16,)), dma((16,)), dma((16,)), dma((2,))],
        compiler_params=pltpu.CompilerParams(collective_id=1, has_side_effects=True),
        name="scatter_grads",
    )(key_part, value_part, query_grad)
    return (
        query_grad[None],
        handed[None],
        key_grad.reshape(1, tok, HD),
        value_grad.reshape(1, tok, HD),
    )


def solution(mesh):
    split = P("pipe", "ctx", None)
    return jax.shard_map(
        on_device,
        mesh=mesh,
        in_specs=(split,) * 5 + (P(), P()),
        out_specs=(split,) * 4,
        check_vma=False,
    )
```

time: 420 us -> 66.3 us (0.16)
  waiting for transfers between devices: 300 us -> 0 us
  matrix products: 78 us -> 0 us
  Pallas kernels: 0 us -> 62.2 us
  between operations: 13.9 us -> 0.66 us
  other arithmetic: 12.8 us -> 0 us
  starting transfers between devices: 6.12 us -> 0 us
    reduce_scatter x2 -> x0, waiting for transfers between devices: 193 us -> none  [the longest x1 105 us: on_device(): lax.psum_scatter(value_terms.astype(jnp.bfloat16), 'ctx', scatter_dimensi...]
    all_gather x2 -> x0, waiting for transfers between devices: 99.3 us -> none  [the longest x1 58.8 us: on_device(): lax.all_gather(key_local, 'ctx', axis=0, tiled=True)]
    dot_general x48 -> x0, matrix products: 78 us -> none  [the longest x16 24.5 us: block_scores(): jnp.einsum('qhd,kd->hqk', query_heads, key_block, preferred_element_type=...]
    pallas_call x0 -> x3, Pallas kernels: none -> 62.2 us  [the longest x1 28.6 us: on_device(): pl.pallas_call(scatter_kernel, out_shape=(own, own, jax.ShapeDtypeStruct(...]
    reduce_sum x42 -> x0, other arithmetic: 7.88 us -> none  [the longest x8 4.15 us: block_stats(): return (new_top, total * jnp.exp(top - new_top) + jnp.sum(weights, axis=2))]
    ppermute x1 -> x0, starting transfers between devices: 5.96 us -> none  [shifted(): return lax.ppermute(x, axis, [(i, (i + by) % count) for i in range(count)])]
    ppermute x1 -> x0, waiting for transfers between devices: 5.93 us -> none  [shifted(): return lax.ppermute(x, axis, [(i, (i + by) % count) for i in range(count)])]
  transfers between devices with their start and end apart: 5 -> 0, of which waited for: 5 -> 0; matrix products, arithmetic and copies ran while one was open for 6% -> 0% of each run, Pallas kernels for 0% -> 0%
where the time goes in v1:
time: 66.3 us; the launch traced here: 65.9 us
  Pallas kernels  62.2 us (94%)
  local copies, waits for them, and re-layouts  3.06 us (5%)
    pallas_call x1, Pallas kernels, on_device(): pl.pallas_call(scatter_kernel, out_shape=(own, own, jax.ShapeDtypeStruct(...  28.6 us
    pallas_call x1, Pallas kernels, on_device(): pl.pallas_call(gather_kernel, out_shape=(full, full), in_specs=[vmem] * 2...  25.7 us
    pallas_call x1, Pallas kernels, on_device(): pl.pallas_call(attend_kernel, out_shape=(jax.ShapeDtypeStruct((tok, HQ *...  7.92 us
    unnamed x7, local copies, waits for them, and re-layouts  3.06 us

profile of v1, /device:TPU:6, one launch (start us, length us, event | category | flops | bytes accessed | tf_op | source)
XLA Modules:
  0.0 65.9 jit_solution(9091522471053798434)
XLA Ops:
  0.6 25.7 %gather_keys_values.1 = (bf16[64,64,128]{2,1,0:T(8,128)(2,1)}, bf16[64,64,128]{2,1,0:T(8,128)(2,1)}) custom-call(bf16[2,64,128]{2,1,0:T(8,128)(2,1)} %bitcast.14, bf16[2,64,128]{2,1,0:T(8,128)(2,1)} %bitcast.15), custom_call_target="tpu_custom_call" | custom-call | tf_op jit(solution)/shard_map/gather_keys_values/pallas_call | solution.py:379
  26.3 7.9 %attend_backward.1 = (bf16[128,1024]{1,0:T(8,128)(2,1)}, bf16[64,64,128]{2,1,0:T(8,128)(2,1)}, bf16[64,64,128]{2,1,0:T(8,128)(2,1)}) custom-call(s32[16]{0:T(128)} %docs.1, s32[32]{0:T(128)} %pairs.1, bf16[128,1024]{1,0:T(8,128)(2,1)} %bitcast.11, bf16[128,1024]{1,0:T(8,128)(2,1)} %bitcast.12, bf16[128,1024]{1,0:T(8,128)(2,1)} %bitcast.13, ...), custom_call_target="tpu_custom_call" | custom-call | tf_op jit(solution)/shard_map/attend_backward/pallas_call | solution.py:388
  34.2 28.6 %scatter_grads.1 = (bf16[2,64,128]{2,1,0:T(8,128)(2,1)}, bf16[2,64,128]{2,1,0:T(8,128)(2,1)}, bf16[128,1024]{1,0:T(8,128)(2,1)}) custom-call(bf16[64,64,128]{2,1,0:T(8,128)(2,1)} %get-tuple-element.15.kp_ref, bf16[64,64,128]{2,1,0:T(8,128)(2,1)} %get-tuple-element.16.vp_ref, bf16[128,1024]{1,0:T(8,128)(2,1)} %get-tuple-element.14.dq_ref), custom_call_target="tpu_custom_call" | custom-call | tf_op jit(solution)/shard_map/scatter_grads/pallas_call | solution.py:406
  62.9 0.0 copy-start.1
  62.9 1.7 %copy.14 = bf16[1,128,1024]{2,1,0:T(8,128)(2,1)} copy(bf16[1,128,1024]{2,1,0:T(8,128)(2,1)} %bitcast.10) | data formatting | bytes 524288
  64.5 0.0 copy-done.1
  64.5 0.0 copy-start
  64.5 0.6 copy.15
  65.2 0.2 copy-done
  65.3 0.6 copy.16
Async XLA Ops:
  62.9 1.7 %copy-start.1 = (bf16[2,64,128]{2,1,0:T(8,128)(2,1)S(1)}, bf16[2,64,128]{2,1,0:T(8,128)(2,1)}, u32[]{:S(2)}) copy-start(bf16[2,64,128]{2,1,0:T(8,128)(2,1)} %get-tuple-element.18) | copy-start | bytes 98308
  64.5 0.8 %copy-start = (bf16[2,64,128]{2,1,0:T(8,128)(2,1)S(1)}, bf16[2,64,128]{2,1,0:T(8,128)(2,1)}, u32[]{:S(2)}) copy-start(bf16[2,64,128]{2,1,0:T(8,128)(2,1)} %get-tuple-element.19) | copy-start | bytes 98308

commit v2 on v1

--- a/solution.py
+++ b/solution.py
@@ -80,45 +80,66 @@
     sent, send = sender(send_sem, recv_sem)
     half = place.core * (SIDE * GROUP)
 
-    def block(d, lo=0, n=2):
-        return full.at[pl.ds(half + slow * GROUP + step(fast, d) * 2 + lo, n)]
-
-    def group(d, lo=0, n=GROUP):
-        return full.at[pl.ds(half + step(slow, d) * GROUP + lo, n)]
+    def block(f, d=0, lo=0, n=2):
+        return full.at[pl.ds(half + step(slow, d) * GROUP + step(fast, f) * 2 + lo, n)]
+
+    def group(d):
+        return full.at[pl.ds(half + step(slow, d) * GROUP, GROUP)]
+
+    def spread(i, f, src=None):
+        src = block(f) if src is None else src
+        send(i, src, block(f), along_slow(1))
+        send(i + 1, src, block(f), along_slow(-1))
+
+    def relay(i, f, toward):
+        send(i, block(f, -toward), block(f, -toward), along_slow(toward))
 
     send(0, own, block(0), along_fast(1))
     send(1, own, block(0), along_fast(-1))
+    spread(4, 0, own)
     mine = pltpu.make_async_copy(own, block(0), own_sem)
     mine.start()
     yield
     sent[0].wait_recv()
-    send(2, block(-1, 0, 1), block(-1, 0, 1), along_fast(1))
+    send(2, block(-1, 0, 0, 1), block(-1, 0, 0, 1), along_fast(1))
+    spread(6, -1)
     yield
     sent[1].wait_recv()
-    send(3, block(1, 1, 1), block(1, 1, 1), along_fast(-1))
-    mine.wait()
+    send(3, block(1, 0, 1, 1), block(1, 0, 1, 1), along_fast(-1))
+    spread(8, 1)
+    yield
+    sent[4].wait_recv()
+    relay(12, 0, 1)
     yield
     sent[2].wait_recv()
     sent[3].wait_recv()
-    send(4, group(0), group(0), along_slow(1))
-    send(5, group(0), group(0), along_slow(-1))
-    send(6, group(0), group(0), place.sibling())
-    yield
-    sent[4].wait_recv()
-    send(7, group(-1, 0, SIDE), group(-1, 0, SIDE), along_slow(1))
-    send(9, group(-1), group(-1), place.sibling())
+    spread(10, 2)
+    mine.wait()
+    send(16, group(0), group(0), place.sibling())
+    yield
+    sent[7].wait_recv()
+    relay(13, -1, -1)
+    yield
+    sent[9].wait_recv()
+    relay(14, 1, -1)
+    yield
+    sent[10].wait_recv()
+    relay(15, 2, 1)
+    sent[6].wait_recv()
+    sent[8].wait_recv()
+    send(17, group(-1), group(-1), place.sibling())
     yield
     sent[5].wait_recv()
-    send(8, group(1, SIDE, SIDE), group(1, SIDE, SIDE), along_slow(-1))
-    send(10, group(1), group(1), place.sibling())
-    yield
-    sent[7].wait_recv()
-    sent[8].wait_recv()
-    send(11, group(2), group(2), place.sibling())
-    yield
-    for i in (6, 9, 10, 11):
+    sent[11].wait_recv()
+    send(18, group(1), group(1), place.sibling())
+    yield
+    for n, f in enumerate((0, -1, 1, 2)):
+        sent[12 + n].wait_recv()
+        send(19 + n, block(f, 2), block(f, 2), place.sibling())
+        yield
+    for i in range(16, 23):
         sent[i].wait_recv()
-    for i in range(12):
+    for i in range(23):
         sent[i].wait_send()
 
 
@@ -142,13 +163,21 @@
 
 
 def scatter_stream(place, fast_is_x, part, out, bufs, send_sem, recv_sem):
-    sib, acc, across_a, across_b, from_low, from_high, line, near_a, near_b, end_low, end_high = bufs
+    sib, acc, across, from_low, from_high, line, near_a, near_b, end_low, end_high = bufs
     fast, slow, along_fast, along_slow = place.order(fast_is_x)
     sent, send = sender(send_sem, recv_sem)
     mine, other = place.core * (SIDE * GROUP), (1 - place.core) * (SIDE * GROUP)
-
-    def at(d, lo=0, n=GROUP):
-        return pl.ds(step(slow, d) * GROUP + lo, n)
+    order = (2, 1, -1, 0)
+    way = (1, -1, -1, 1)
+
+    def at(d):
+        return pl.ds(step(slow, d) * GROUP, GROUP)
+
+    def block(d, n):
+        return pl.ds(step(slow, d) * GROUP + step(fast, order[n]) * 2, 2)
+
+    def slot(n):
+        return pl.ds(2 * n, 2)
 
     def merge(d):
         acc[at(d)] = add(part[pl.ds(mine + step(slow, d) * GROUP, GROUP)], sib[at(d)])
@@ -158,82 +187,76 @@
     yield
     sent[0].wait_recv()
     merge(2)
-    send(4, acc.at[at(2, 0, SIDE)], across_a, along_slow(1))
-    send(5, acc.at[at(2, SIDE, SIDE)], across_b, along_slow(-1))
+    for n in range(4):
+        send(4 + n, acc.at[block(2, n)], across.at[slot(n)], along_slow(way[n]))
     yield
     sent[1].wait_recv()
     merge(1)
-    send(6, acc.at[at(1, SIDE, SIDE)], from_low.at[pl.ds(SIDE, SIDE)], along_slow(1))
+    for n in (1, 2):
+        send(8 + n, acc.at[block(1, n)], from_low.at[slot(n)], along_slow(1))
     yield
     sent[2].wait_recv()
     merge(-1)
-    send(7, acc.at[at(-1, 0, SIDE)], from_high.at[pl.ds(0, SIDE)], along_slow(-1))
+    for n in (0, 3):
+        send(8 + n, acc.at[block(-1, n)], from_high.at[slot(n)], along_slow(-1))
     yield
     sent[3].wait_recv()
     merge(0)
     yield
-    sent[4].wait_recv()
-    acc[at(1, 0, SIDE)] = add(acc[at(1, 0, SIDE)], across_a[...])
-    send(8, acc.at[at(1, 0, SIDE)], from_low.at[pl.ds(0, SIDE)], along_slow(1))
-    yield
-    sent[5].wait_recv()
-    acc[at(-1, SIDE, SIDE)] = add(acc[at(-1, SIDE, SIDE)], across_b[...])
-    send(9, acc.at[at(-1, SIDE, SIDE)], from_high.at[pl.ds(SIDE, SIDE)], along_slow(-1))
-    yield
-    for i in (6, 7, 8, 9):
+    for n in range(4):
+        sent[4 + n].wait_recv()
+        acc[block(way[n], n)] = add(acc[block(way[n], n)], across[slot(n)])
+        target = from_low if way[n] == 1 else from_high
+        send(12 + n, acc.at[block(way[n], n)], target.at[slot(n)], along_slow(way[n]))
+        yield
+
+    def settle(n):
+        sent[8 + n].wait_recv()
+        sent[12 + n].wait_recv()
+        line[slot(n)] = add(acc[block(0, n)], from_low[slot(n)], from_high[slot(n)])
+
+    settle(0)
+    send(16, line.at[pl.ds(0, 1)], near_a, along_fast(1))
+    send(17, line.at[pl.ds(1, 1)], near_b, along_fast(-1))
+    yield
+    settle(1)
+    send(18, line.at[pl.ds(3, 1)], end_low.at[pl.ds(1, 1)], along_fast(1))
+    yield
+    settle(2)
+    send(19, line.at[pl.ds(4, 1)], end_high.at[pl.ds(0, 1)], along_fast(-1))
+    yield
+    sent[16].wait_recv()
+    line[pl.ds(2, 1)] = add(line[pl.ds(2, 1)], near_a[...])
+    send(20, line.at[pl.ds(2, 1)], end_low.at[pl.ds(0, 1)], along_fast(1))
+    yield
+    sent[17].wait_recv()
+    line[pl.ds(5, 1)] = add(line[pl.ds(5, 1)], near_b[...])
+    send(21, line.at[pl.ds(5, 1)], end_high.at[pl.ds(1, 1)], along_fast(-1))
+    yield
+    settle(3)
+    for i in (18, 19, 20, 21):
         sent[i].wait_recv()
-    line[...] = add(acc[at(0)], from_low[...], from_high[...])
-
-    def one(d, lo, n=1):
-        return pl.ds(step(fast, d) * 2 + lo, n)
-
-    send(10, line.at[one(2, 0)], near_a, along_fast(1))
-    send(11, line.at[one(2, 1)], near_b, along_fast(-1))
-    send(12, line.at[one(1, 1)], end_low.at[pl.ds(1, 1)], along_fast(1))
-    send(13, line.at[one(-1, 0)], end_high.at[pl.ds(0, 1)], along_fast(-1))
-    yield
-    sent[10].wait_recv()
-    line[one(1, 0)] = add(line[one(1, 0)], near_a[...])
-    send(14, line.at[one(1, 0)], end_low.at[pl.ds(0, 1)], along_fast(1))
-    yield
-    sent[11].wait_recv()
-    line[one(-1, 1)] = add(line[one(-1, 1)], near_b[...])
-    send(15, line.at[one(-1, 1)], end_high.at[pl.ds(1, 1)], along_fast(-1))
-    yield
-    for i in (12, 13, 14, 15):
-        sent[i].wait_recv()
-    out[...] = add(line[one(0, 0, 2)], end_low[...], end_high[...])
-    for i in range(16):
+    out[...] = add(line[slot(3)], end_low[...], end_high[...])
+    for i in range(22):
         sent[i].wait_send()
 
 
-SCATTER_BUFS = (SIDE * GROUP, SIDE * GROUP, SIDE, SIDE, GROUP, GROUP, GROUP, 1, 1, 2, 2)
-
-
-def scatter_kernel(kp_ref, vp_ref, dq_ref, kg_ref, vg_ref, handed_ref, *scratch):
+SCATTER_BUFS = (SIDE * GROUP, SIDE * GROUP, GROUP, GROUP, GROUP, GROUP, 1, 1, 2, 2)
+
+
+def scatter_kernel(kp_ref, vp_ref, kg_ref, vg_ref, *scratch):
     count = len(SCATTER_BUFS)
     k_bufs, v_bufs = scratch[:count], scratch[count : 2 * count]
-    k_send, k_recv, v_send, v_recv, hand_sem = scratch[2 * count :]
+    k_send, k_recv, v_send, v_recv = scratch[2 * count :]
     place = Place()
-    section, sections = lax.axis_index("pipe"), lax.axis_size("pipe")
-    below = lax.rem(section + sections - 1, sections)
-    above = lax.rem(section + 1, sections)
     barrier = pltpu.get_barrier_semaphore()
     for device in place.neighbours():
         pl.semaphore_signal(barrier, inc=1, device_id={"ctx": device}, device_id_type=MESH)
-    for device in (below, above):
-        pl.semaphore_signal(barrier, inc=1, device_id={"pipe": device}, device_id_type=MESH)
-    pl.semaphore_wait(barrier, 7)
-    hand = pltpu.make_async_remote_copy(
-        src_ref=dq_ref, dst_ref=handed_ref, send_sem=hand_sem.at[0], recv_sem=hand_sem.at[1],
-        device_id={"pipe": below}, device_id_type=MESH,
-    )
-    hand.start()
+    pl.semaphore_wait(barrier, 5)
     in_turn(
         scatter_stream(place, True, kp_ref, kg_ref, k_bufs, k_send, k_recv),
         scatter_stream(place, False, vp_ref, vg_ref, v_bufs, v_send, v_recv),
     )
-    hand.wait()
 
 
 def dot(a, b, over):
@@ -381,7 +404,7 @@
         out_shape=(full, full),
         in_specs=[vmem] * 2,
         out_specs=(vmem, vmem),
-        scratch_shapes=[dma((2,)), dma((12,)), dma((12,)), dma((12,)), dma((12,))],
+        scratch_shapes=[dma((2,))] + [dma((23,))] * 4,
         compiler_params=pltpu.CompilerParams(collective_id=0, has_side_effects=True),
         name="gather_keys_values",
     )(keys.reshape(2, ST, HD), values.reshape(2, ST, HD))
@@ -403,15 +426,18 @@
         name="attend_backward",
     )(doc_lengths, pair_of_rank, queries[0], attn_out[0], grad_out[0], all_keys, all_values)
     bufs = [pltpu.VMEM((n, ST, HD), BF16) for n in SCATTER_BUFS]
-    key_grad, value_grad, handed = pl.pallas_call(
+    sections = lax.axis_size("pipe")
+    handed = lax.ppermute(query_grad, "pipe", [(i, (i - 1) % sections) for i in range(sections)])
+    key_grad, value_grad = pl.pallas_call(
         scatter_kernel,
-        out_shape=(own, own, jax.ShapeDtypeStruct((tok, HQ * HD), BF16)),
-        in_specs=[vmem, vmem, hbm],
-        out_specs=(vmem, vmem, hbm),
-        scratch_shapes=bufs + bufs + [dma((16,)), dma((16,)), dma((16,)), dma((16,)), dma((2,))],
+        out_shape=(own, own),
+        in_specs=[vmem] * 2,
+        out_specs=(vmem,) * 2,
+        scratch_shapes=bufs + bufs + [dma((22,))] * 4,
         compiler_params=pltpu.CompilerParams(collective_id=1, has_side_effects=True),
+        cost_estimate=pl.CostEstimate(flops=2**30, bytes_accessed=2**26, transcendentals=0),
         name="scatter_grads",
-    )(key_part, value_part, query_grad)
+    )(key_part, value_part)
     return (
         query_grad[None],
         handed[None],

time: 66.3 us -> 66.8 us (level)
  starting transfers between devices: 0 us -> 8.69 us
  Pallas kernels: 62.2 us -> 54.4 us
  local copies, waits for them, and re-layouts: 3.06 us -> 2.13 us
    ppermute x0 -> x1, starting transfers between devices: none -> 8.69 us  [on_device(): lax.ppermute(query_grad, 'pipe', [(i, (i - 1) % sections) for i in range(...]
    pallas_call x1, Pallas kernels: 28.6 us -> 20.2 us  [on_device(): pl.pallas_call(scatter_kernel, out_shape=(own, own), in_specs=[vmem] * 2,...]
    pallas_call x1, Pallas kernels: 7.92 us -> 11 us  [on_device(): pl.pallas_call(attend_kernel, out_shape=(jax.ShapeDtypeStruct((tok, HQ *...]
    pallas_call x1, Pallas kernels: 25.7 us -> 23.2 us  [on_device(): pl.pallas_call(gather_kernel, out_shape=(full, full), in_specs=[vmem] * 2...]
    unnamed x7, local copies, waits for them, and re-layouts: 3.06 us -> 2.13 us
  transfers between devices with their start and end apart: 0 -> 1, of which waited for: 0 -> 0; matrix products, arithmetic and copies ran while one was open for 0% -> 0% of each run, Pallas kernels for 0% -> 31%
where the time goes in v2:
time: 66.8 us; the launch traced here: 65.9 us
  Pallas kernels  54.4 us (81%)
  starting transfers between devices  8.69 us (13%)
  local copies, waits for them, and re-layouts  2.13 us (3%)
  between operations  0.67 us (1%)
    pallas_call x1, Pallas kernels, on_device(): pl.pallas_call(gather_kernel, out_shape=(full, full), in_specs=[vmem] * 2...  23.2 us
    pallas_call x1, Pallas kernels, on_device(): pl.pallas_call(scatter_kernel, out_shape=(own, own), in_specs=[vmem] * 2,...  20.2 us
    pallas_call x1, Pallas kernels, on_device(): pl.pallas_call(attend_kernel, out_shape=(jax.ShapeDtypeStruct((tok, HQ *...  11 us
    ppermute x1, starting transfers between devices, on_device(): lax.ppermute(query_grad, 'pipe', [(i, (i - 1) % sections) for i in range(...  8.69 us
    unnamed x7, local copies, waits for them, and re-layouts  2.13 us
  transfers between devices with their start and end apart: 1, of which 0 were waited for; matrix products, arithmetic and copies ran while one was open for 0% of the time, Pallas kernels for 31%

profile of v2, /device:TPU:6, one launch (start us, length us, event | category | flops | bytes accessed | tf_op | source)
XLA Modules:
  0.0 65.9 jit_solution(4399193175179289405)
XLA Ops:
  0.6 23.2 %gather_keys_values.1 = (bf16[64,64,128]{2,1,0:T(8,128)(2,1)}, bf16[64,64,128]{2,1,0:T(8,128)(2,1)}) custom-call(bf16[2,64,128]{2,1,0:T(8,128)(2,1)} %bitcast.13, bf16[2,64,128]{2,1,0:T(8,128)(2,1)} %bitcast.14), custom_call_target="tpu_custom_call" | custom-call | tf_op jit(solution)/shard_map/gather_keys_values/pallas_call | solution.py:402
  23.9 11.0 %attend_backward.1 = (bf16[128,1024]{1,0:T(8,128)(2,1)}, bf16[64,64,128]{2,1,0:T(8,128)(2,1)}, bf16[64,64,128]{2,1,0:T(8,128)(2,1)}) custom-call(s32[16]{0:T(128)} %docs.1, s32[32]{0:T(128)} %pairs.1, bf16[128,1024]{1,0:T(8,128)(2,1)} %bitcast.10, bf16[128,1024]{1,0:T(8,128)(2,1)} %bitcast.11, bf16[128,1024]{1,0:T(8,128)(2,1)} %bitcast.12, ...), custom_call_target="tpu_custom_call" | custom-call | tf_op jit(solution)/shard_map/attend_backward/pallas_call | solution.py:411
  34.8 8.7 %collective-permute-start = (bf16[128,1024]{1,0:T(8,128)(2,1)}, bf16[128,1024]{1,0:T(8,128)(2,1)S(1)}, u32[]{:S(2)}, u32[]{:S(2)}) collective-permute-start(bf16[128,1024]{1,0:T(8,128)(2,1)} %get-tuple-element.13), channel_id=1, source_target_pairs={{0,480},{32,0},{64,32},{96,64},{128,96},{160,128},{192,160},{224,1... | collective-permute-start | bytes 786440 | tf_op jit(solution)/shard_map/ppermute | solution.py:430
  43.5 20.2 %scatter_grads.1 = (bf16[2,64,128]{2,1,0:T(8,128)(2,1)}, bf16[2,64,128]{2,1,0:T(8,128)(2,1)}) custom-call(bf16[64,64,128]{2,1,0:T(8,128)(2,1)} %get-tuple-element.14.kp_ref, bf16[64,64,128]{2,1,0:T(8,128)(2,1)} %get-tuple-element.15.vp_ref), custom_call_target="tpu_custom_call" | custom-call | flops 1073741824 | bytes 67108864 | tf_op jit(solution)/shard_map/scatter_grads/pallas_call | solution.py:431
  63.7 0.0 collective-permute-done
  63.8 0.0 copy-start.1
  63.8 0.7 %copy.14 = bf16[1,128,1024]{2,1,0:T(8,128)(2,1)} copy(bf16[1,128,1024]{2,1,0:T(8,128)(2,1)S(1)} %bitcast.9) | data formatting | bytes 524288
  64.5 0.0 copy-done.1
  64.5 0.0 copy-start
  64.5 0.6 copy.15
  65.1 0.2 copy-done
  65.3 0.6 copy.16
Async XLA Ops:
  34.8 28.9 %collective-permute-start = (bf16[128,1024]{1,0:T(8,128)(2,1)}, bf16[128,1024]{1,0:T(8,128)(2,1)S(1)}, u32[]{:S(2)}, u32[]{:S(2)}) collective-permute-start(bf16[128,1024]{1,0:T(8,128)(2,1)} %get-tuple-element.13), channel_id=1, source_target_pairs={{0,480},{32,0},{64,32},{96,64},{128,96},{160,128},{192,160},{224,1... | collective-permute-start | bytes 786440 | tf_op jit(solution)/shard_map/ppermute | solution.py:430
  63.8 0.8 %copy-start.1 = (bf16[2,64,128]{2,1,0:T(8,128)(2,1)S(1)}, bf16[2,64,128]{2,1,0:T(8,128)(2,1)}, u32[]{:S(2)}) copy-start(bf16[2,64,128]{2,1,0:T(8,128)(2,1)} %get-tuple-element.16) | copy-start | bytes 98308
  64.5 0.8 %copy-start = (bf16[2,64,128]{2,1,0:T(8,128)(2,1)S(1)}, bf16[2,64,128]{2,1,0:T(8,128)(2,1)}, u32[]{:S(2)}) copy-start(bf16[2,64,128]{2,1,0:T(8,128)(2,1)} %get-tuple-element.17) | copy-start | bytes 98308

commit v3 on v2

--- a/solution.py
+++ b/solution.py
@@ -15,6 +15,7 @@
 STRETCHES = 2 * RANKS
 WIN = 18
 CHUNK = 384
+PART = CHUNK // ST
 CHUNKS = WIN * ST // CHUNK
 ROWS = HQ * ST
 GROUP = 2 * SIDE
@@ -162,11 +163,10 @@
     return total.astype(BF16)
 
 
-def scatter_stream(place, fast_is_x, part, out, bufs, send_sem, recv_sem):
-    sib, acc, across, from_low, from_high, line, near_a, near_b, end_low, end_high = bufs
+def scatter_stream(place, fast_is_x, term, out, bufs, send_sem, recv_sem):
+    outgoing, sib, acc, across, from_low, from_high, line, near_a, near_b, end_low, end_high = bufs
     fast, slow, along_fast, along_slow = place.order(fast_is_x)
     sent, send = sender(send_sem, recv_sem)
-    mine, other = place.core * (SIDE * GROUP), (1 - place.core) * (SIDE * GROUP)
     order = (2, 1, -1, 0)
     way = (1, -1, -1, 1)
 
@@ -179,12 +179,24 @@
     def slot(n):
         return pl.ds(2 * n, 2)
 
+    def own_term(core, d, n):
+        line_at, half = step(slow, d), n % 2
+        y, x = (line_at, n // 2) if fast_is_x else (n // 2, line_at)
+        return term((y * SIDE + x) * 2 + core, half)
+
+    def fill(d):
+        for n in range(GROUP):
+            outgoing[step(slow, d) * GROUP + n] = own_term(1 - place.core, d, n)
+
     def merge(d):
-        acc[at(d)] = add(part[pl.ds(mine + step(slow, d) * GROUP, GROUP)], sib[at(d)])
+        for n in range(GROUP):
+            index = step(slow, d) * GROUP + n
+            acc[index] = add(own_term(place.core, d, n), sib[index])
 
     for i, d in enumerate((2, 1, -1, 0)):
-        send(i, part.at[pl.ds(other + step(slow, d) * GROUP, GROUP)], sib.at[at(d)], place.sibling())
-    yield
+        fill(d)
+        send(i, outgoing.at[at(d)], sib.at[at(d)], place.sibling())
+        yield
     sent[0].wait_recv()
     merge(2)
     for n in range(4):
@@ -241,37 +253,37 @@
         sent[i].wait_send()
 
 
-SCATTER_BUFS = (SIDE * GROUP, SIDE * GROUP, GROUP, GROUP, GROUP, GROUP, 1, 1, 2, 2)
-
-
-def scatter_kernel(kp_ref, vp_ref, kg_ref, vg_ref, *scratch):
+SCATTER_BUFS = (SIDE * GROUP, SIDE * GROUP, SIDE * GROUP, GROUP, GROUP, GROUP, GROUP, 1, 1, 2, 2)
+
+
+def dot(a, b, over):
+    return lax.dot_general(a, b, ((over[:1], over[1:]), ((), ())), preferred_element_type=F32)
+
+
+def attend_scatter_kernel(
+    docs, pairs, q_ref, o_ref, g_ref, k_ref, v_ref, dq_ref, handed_ref, kg_ref, vg_ref,
+    rank_of_pair, q_rows, g_rows, key_win, value_win, work, key_terms, value_terms, *scratch,
+):
     count = len(SCATTER_BUFS)
     k_bufs, v_bufs = scratch[:count], scratch[count : 2 * count]
-    k_send, k_recv, v_send, v_recv = scratch[2 * count :]
+    k_send, k_recv, v_send, v_recv, hand_sem = scratch[2 * count :]
     place = Place()
+    section, sections = lax.axis_index("pipe"), lax.axis_size("pipe")
+    below = lax.rem(section + sections - 1, sections)
+    above = lax.rem(section + 1, sections)
     barrier = pltpu.get_barrier_semaphore()
     for device in place.neighbours():
         pl.semaphore_signal(barrier, inc=1, device_id={"ctx": device}, device_id_type=MESH)
-    pl.semaphore_wait(barrier, 5)
-    in_turn(
-        scatter_stream(place, True, kp_ref, kg_ref, k_bufs, k_send, k_recv),
-        scatter_stream(place, False, vp_ref, vg_ref, v_bufs, v_send, v_recv),
-    )
-
-
-def dot(a, b, over):
-    return lax.dot_general(a, b, ((over[:1], over[1:]), ((), ())), preferred_element_type=F32)
-
-
-def attend_kernel(
-    docs, pairs, q_ref, o_ref, g_ref, k_ref, v_ref, dq_ref, kp_ref, vp_ref,
-    rank_of_pair, q_rows, g_rows, key_win, value_win, work, key_terms, value_terms,
-):
+    for device in (below, above):
+        pl.semaphore_signal(barrier, inc=1, device_id={"pipe": device}, device_id_type=MESH)
     scale = 1.0 / math.sqrt(HD)
     pair = pairs[lax.axis_index("ctx")]
 
-    def note(r, carry):
-        rank_of_pair[pairs[r]] = r
+    def note(p, carry):
+        found = jnp.int32(0)
+        for r in range(RANKS):
+            found = jnp.maximum(found, jnp.where(pairs[r] == p, r, 0))
+        rank_of_pair[p] = found
         return carry
 
     lax.fori_loop(0, RANKS, note, 0)
@@ -284,8 +296,9 @@
         size = SIDE * SIDE
         return (core * size + chip) * 2 + late, (core * size + turned) * 2 + late
 
-    kp_ref[...] = jnp.zeros_like(kp_ref)
-    vp_ref[...] = jnp.zeros_like(vp_ref)
+    for which in range(2):
+        key_terms[which, WIN] = jnp.zeros((ST, HD), F32)
+        value_terms[which, WIN] = jnp.zeros((ST, HD), F32)
     bases = (pair, STRETCHES - 1 - pair)
     lane = lax.rem(lax.broadcasted_iota(jnp.int32, (1, ROWS), 1), ST)
     for which in range(2):
@@ -308,13 +321,11 @@
             key_win[j * ST : (j + 1) * ST] = k_ref[k_at]
             value_win[j * ST : (j + 1) * ST] = v_ref[v_at]
         position = base * ST + lane
-        start, first, end = jnp.zeros_like(position), jnp.int32(0), jnp.int32(0)
+        start, end = jnp.zeros_like(position), jnp.int32(0)
         for d in range(docs.shape[0]):
             end = end + docs[d]
             start = jnp.where(position >= end, end, start)
-            first = jnp.where(base * ST >= end, end, first)
         low, high = start - lowest, position - lowest
-        begin = (first - lowest) // CHUNK
 
         def scores(c, top):
             at = pl.multiple_of(c * CHUNK, CHUNK)
@@ -324,71 +335,59 @@
             work[c] = found
             return jnp.maximum(top, jnp.max(found, axis=0, keepdims=True))
 
-        top = lax.fori_loop(begin, CHUNKS, scores, jnp.full((1, ROWS), NEG, F32))
+        top = lax.fori_loop(0, CHUNKS, scores, jnp.full((1, ROWS), NEG, F32))
 
         def weigh(c, total):
             weights = jnp.exp2((work[c] - top) * (scale * math.log2(math.e)))
             work[c] = weights
             return total + jnp.sum(weights, axis=0, keepdims=True)
 
-        total = lax.fori_loop(begin, CHUNKS, weigh, jnp.zeros((1, ROWS), F32))
+        total = lax.fori_loop(0, CHUNKS, weigh, jnp.zeros((1, ROWS), F32))
         inverse = 1.0 / total
 
         def grads(c, dq_sum):
             at = pl.multiple_of(c * CHUNK, CHUNK)
             probs = work[c] * inverse
-            value_terms[which, pl.ds(at, CHUNK)] = dot(probs.astype(BF16), g_rows[...], (1, 0))
+            value_terms[which, pl.ds(c * PART, PART)] = dot(probs.astype(BF16), g_rows[...], (1, 0)).reshape(PART, ST, HD)
             dprobs = dot(value_win[pl.ds(at, CHUNK)], g_rows[...], (1, 1))
             dscores = (probs * (dprobs - delta)).astype(BF16)
-            key_terms[which, pl.ds(at, CHUNK)] = dot(dscores, q_rows[...], (1, 0)) * scale
+            key_terms[which, pl.ds(c * PART, PART)] = (dot(dscores, q_rows[...], (1, 0)) * scale).reshape(PART, ST, HD)
             turned = jnp.transpose(key_win[pl.ds(at, CHUNK)])
             return dq_sum + dot(turned, dscores, (1, 0))
 
-        dq_sum = lax.fori_loop(begin, CHUNKS, grads, jnp.zeros((HD, ROWS), F32))
+        dq_sum = lax.fori_loop(0, CHUNKS, grads, jnp.zeros((HD, ROWS), F32))
         dq_rows = (jnp.transpose(dq_sum) * scale).astype(BF16)
         for h in range(HQ):
             dq_ref[rows, h * HD : (h + 1) * HD] = dq_rows[h * ST : (h + 1) * ST]
 
-        def clear(c, carry):
-            at = pl.multiple_of(c * CHUNK, CHUNK)
-            key_terms[which, pl.ds(at, CHUNK)] = jnp.zeros((CHUNK, HD), F32)
-            value_terms[which, pl.ds(at, CHUNK)] = jnp.zeros((CHUNK, HD), F32)
-            return carry
-
-        lax.fori_loop(0, begin, clear, 0)
-
     early, late = bases[0] - (WIN - 1), bases[1] - (WIN - 1)
 
-    def put_early(j, carry):
-        t = early + j
-
-        @pl.when((t >= 0) & (t < late))
-        def _():
-            k_at, v_at = places(t)
-            at = pl.multiple_of(j * ST, ST)
-            kp_ref[k_at] = key_terms[0, pl.ds(at, ST)].astype(BF16)
-            vp_ref[v_at] = value_terms[0, pl.ds(at, ST)].astype(BF16)
-
-        return carry
-
-    lax.fori_loop(0, WIN, put_early, 0)
-
-    def put_late(j, carry):
-        t = late + j
-        k_at, v_at = places(t)
-        at = pl.multiple_of(j * ST, ST)
-        shared = t - early
-        both = (shared >= 0) & (shared < WIN)
-        near = pl.multiple_of(jnp.clip(shared, 0, WIN - 1) * ST, ST)
-        kp_ref[k_at] = (
-            key_terms[1, pl.ds(at, ST)] + jnp.where(both, key_terms[0, pl.ds(near, ST)], 0.0)
-        ).astype(BF16)
-        vp_ref[v_at] = (
-            value_terms[1, pl.ds(at, ST)] + jnp.where(both, value_terms[0, pl.ds(near, ST)], 0.0)
-        ).astype(BF16)
-        return carry
-
-    lax.fori_loop(0, WIN, put_late, 0)
+    def within(j):
+        return jnp.where((j >= 0) & (j < WIN), j, WIN)
+
+    def term_of(terms):
+        def term(rank, half):
+            t = pairs[rank] if half == 0 else STRETCHES - 1 - pairs[rank]
+            return (terms[0, within(t - early)] + terms[1, within(t - late)]).astype(BF16)
+
+        return term
+
+    pl.semaphore_wait(barrier, 7)
+    hand = pltpu.make_async_remote_copy(
+        src_ref=dq_ref, dst_ref=handed_ref, send_sem=hand_sem.at[0], recv_sem=hand_sem.at[1],
+        device_id={"pipe": below}, device_id_type=MESH,
+    )
+    hand.start()
+    in_turn(
+        scatter_stream(place, True, term_of(key_terms), kg_ref, k_bufs, k_send, k_recv),
+        scatter_stream(place, False, term_of(value_terms), vg_ref, v_bufs, v_send, v_recv),
+    )
+    hand.wait()
+
+
+def finish_kernel(*refs):
+    for source, target in zip(refs[:4], refs[4:]):
+        target[...] = source[...]
 
 
 def on_device(queries, keys, values, attn_out, grad_out, doc_lengths, pair_of_rank):
@@ -408,11 +407,13 @@
         compiler_params=pltpu.CompilerParams(collective_id=0, has_side_effects=True),
         name="gather_keys_values",
     )(keys.reshape(2, ST, HD), values.reshape(2, ST, HD))
-    query_grad, key_part, value_part = pl.pallas_call(
-        attend_kernel,
-        out_shape=(jax.ShapeDtypeStruct((tok, HQ * HD), BF16), full, full),
+    bufs = [pltpu.VMEM((n, ST, HD), BF16) for n in SCATTER_BUFS]
+    wide = jax.ShapeDtypeStruct((tok, HQ * HD), BF16)
+    results = pl.pallas_call(
+        attend_scatter_kernel,
+        out_shape=(wide, wide, own, own),
         in_specs=[smem] * 2 + [vmem] * 5,
-        out_specs=(vmem,) * 3,
+        out_specs=(vmem, hbm, vmem, vmem),
         scratch_shapes=[
             pltpu.SMEM((RANKS,), jnp.int32),
             pltpu.VMEM((ROWS, HD), BF16),
@@ -420,24 +421,23 @@
             pltpu.VMEM((WIN * ST, HD), BF16),
             pltpu.VMEM((WIN * ST, HD), BF16),
             pltpu.VMEM((CHUNKS, CHUNK, ROWS), F32),
-            pltpu.VMEM((2, WIN * ST, HD), F32),
-            pltpu.VMEM((2, WIN * ST, HD), F32),
-        ],
-        name="attend_backward",
+            pltpu.VMEM((2, WIN + 1, ST, HD), F32),
+            pltpu.VMEM((2, WIN + 1, ST, HD), F32),
+        ]
+        + bufs
+        + bufs
+        + [dma((22,))] * 4
+        + [dma((2,))],
+        compiler_params=pltpu.CompilerParams(collective_id=1, has_side_effects=True),
+        name="attend_scatter",
     )(doc_lengths, pair_of_rank, queries[0], attn_out[0], grad_out[0], all_keys, all_values)
-    bufs = [pltpu.VMEM((n, ST, HD), BF16) for n in SCATTER_BUFS]
-    sections = lax.axis_size("pipe")
-    handed = lax.ppermute(query_grad, "pipe", [(i, (i - 1) % sections) for i in range(sections)])
-    key_grad, value_grad = pl.pallas_call(
-        scatter_kernel,
-        out_shape=(own, own),
-        in_specs=[vmem] * 2,
-        out_specs=(vmem,) * 2,
-        scratch_shapes=bufs + bufs + [dma((22,))] * 4,
-        compiler_params=pltpu.CompilerParams(collective_id=1, has_side_effects=True),
-        cost_estimate=pl.CostEstimate(flops=2**30, bytes_accessed=2**26, transcendentals=0),
-        name="scatter_grads",
-    )(key_part, value_part)
+    query_grad, handed, key_grad, value_grad = pl.pallas_call(
+        finish_kernel,
+        out_shape=(wide, wide, own, own),
+        in_specs=[vmem] * 4,
+        out_specs=(vmem,) * 4,
+        name="finish",
+    )(*results)
     return (
         query_grad[None],
         handed[None],

time: 66.8 us -> 54.8 us (0.82); the launches traced: 65.9 us -> 54.6 us
  starting transfers between devices: 8.69 us -> 0 us
  local copies, waits for them, and re-layouts: 2.13 us -> 0 us
    ppermute x1 -> x0, starting transfers between devices: 8.69 us -> none  [on_device(): lax.ppermute(query_grad, 'pipe', [(i, (i - 1) % sections) for i in range(...]
    unnamed x7 -> x0, local copies, waits for them, and re-layouts: 2.13 us -> none
  transfers between devices with their start and end apart: 1 -> 0, of which waited for: 0 -> 0; matrix products, arithmetic and copies ran while one was open for 0% -> 0% of each run, Pallas kernels for 31% -> 0%
where the time goes in v3:
time: 54.8 us; the launch traced here: 54.6 us
  Pallas kernels  53.9 us (98%)
  between operations  0.65 us (1%)
    pallas_call x1, Pallas kernels, on_device(): pl.pallas_call(attend_scatter_kernel, out_shape=(wide, wide, own, own), i...  28.8 us
    pallas_call x1, Pallas kernels, on_device(): pl.pallas_call(gather_kernel, out_shape=(full, full), in_specs=[vmem] * 2...  23.3 us
    pallas_call x1, Pallas kernels, on_device(): pl.pallas_call(finish_kernel, out_shape=(wide, wide, own, own), in_specs=...  1.85 us

profile of v3, /device:TPU:6, one launch (start us, length us, event | category | flops | bytes accessed | tf_op | source)
XLA Modules:
  0.0 54.6 jit_solution(2936591135967290155)
XLA Ops:
  0.6 23.3 %gather_keys_values.1 = (bf16[64,64,128]{2,1,0:T(8,128)(2,1)}, bf16[64,64,128]{2,1,0:T(8,128)(2,1)}) custom-call(bf16[2,64,128]{2,1,0:T(8,128)(2,1)} %bitcast.12, bf16[2,64,128]{2,1,0:T(8,128)(2,1)} %bitcast.13), custom_call_target="tpu_custom_call" | custom-call | tf_op jit(solution)/shard_map/gather_keys_values/pallas_call | solution.py:401
  23.9 28.8 %attend_scatter.1 = (bf16[128,1024]{1,0:T(8,128)(2,1)}, bf16[128,1024]{1,0:T(8,128)(2,1)}, bf16[2,64,128]{2,1,0:T(8,128)(2,1)}, bf16[2,64,128]{2,1,0:T(8,128)(2,1)}) custom-call(s32[16]{0:T(128)} %docs.1, s32[32]{0:T(128)} %pairs.1, bf16[128,1024]{1,0:T(8,128)(2,1)} %bitcast.9, bf16[128,1024]{1,0:T(8,128)(2,1)} %bitcast.10, bf16[128,1024]{1,0:T(8,128)(2,1)} %bitcast.11, ...), custom_call_target="tpu_custom_call" | custom-call | tf_op jit(solution)/shard_map/attend_scatter/pallas_call | solution.py:412
  52.7 1.9 %finish.1 = (bf16[128,1024]{1,0:T(8,128)(2,1)}, bf16[128,1024]{1,0:T(8,128)(2,1)}, bf16[2,64,128]{2,1,0:T(8,128)(2,1)}, bf16[2,64,128]{2,1,0:T(8,128)(2,1)}) custom-call(bf16[128,1024]{1,0:T(8,128)(2,1)} %get-tuple-element.16.refs_0_, bf16[128,1024]{1,0:T(8,128)(2,1)} %get-tuple-element.17.refs_1_, bf16[2,64,128]{2,1,0:T(8,128)(2,1)} %get-tuple-element.18.refs_2_, ...), custom_call_target="tpu_custom_call" | custom-call | tf_op jit(solution)/shard_map/finish/pallas_call | solution.py:434

commit v4 on v3

--- a/solution.py
+++ b/solution.py
@@ -42,7 +42,8 @@
         return (self.y * SIDE + self.x) * 2 + 1 - self.core
 
     def neighbours(self):
-        return [self.sibling(), self.at(1, 0), self.at(-1, 0), self.at(0, 1), self.at(0, -1)]
+        steps = [(1, 0), (-1, 0), (2, 0), (0, 1), (0, -1), (0, 2)]
+        return [self.sibling()] + [self.at(dx, dy) for dx, dy in steps]
 
     def order(self, fast_is_x):
         if fast_is_x:
@@ -81,8 +82,8 @@
     sent, send = sender(send_sem, recv_sem)
     half = place.core * (SIDE * GROUP)
 
-    def block(f, d=0, lo=0, n=2):
-        return full.at[pl.ds(half + step(slow, d) * GROUP + step(fast, f) * 2 + lo, n)]
+    def block(f, d=0):
+        return full.at[pl.ds(half + step(slow, d) * GROUP + step(fast, f) * 2, 2)]
 
     def group(d):
         return full.at[pl.ds(half + step(slow, d) * GROUP, GROUP)]
@@ -97,24 +98,23 @@
 
     send(0, own, block(0), along_fast(1))
     send(1, own, block(0), along_fast(-1))
+    send(2, own, block(0), along_fast(2))
     spread(4, 0, own)
     mine = pltpu.make_async_copy(own, block(0), own_sem)
     mine.start()
     yield
     sent[0].wait_recv()
-    send(2, block(-1, 0, 0, 1), block(-1, 0, 0, 1), along_fast(1))
     spread(6, -1)
     yield
     sent[1].wait_recv()
-    send(3, block(1, 0, 1, 1), block(1, 0, 1, 1), along_fast(-1))
     spread(8, 1)
     yield
     sent[4].wait_recv()
     relay(12, 0, 1)
     yield
     sent[2].wait_recv()
-    sent[3].wait_recv()
     spread(10, 2)
+    send(15, block(2), block(2), along_slow(2))
     mine.wait()
     send(16, group(0), group(0), place.sibling())
     yield
@@ -124,10 +124,9 @@
     sent[9].wait_recv()
     relay(14, 1, -1)
     yield
-    sent[10].wait_recv()
-    relay(15, 2, 1)
     sent[6].wait_recv()
     sent[8].wait_recv()
+    sent[10].wait_recv()
     send(17, group(-1), group(-1), place.sibling())
     yield
     sent[5].wait_recv()
@@ -140,8 +139,8 @@
         yield
     for i in range(16, 23):
         sent[i].wait_recv()
-    for i in range(23):
-        sent[i].wait_send()
+    for copy in sent.values():
+        copy.wait_send()
 
 
 def gather_kernel(k_ref, v_ref, gk_ref, gv_ref, own_sem, k_send, k_recv, v_send, v_recv):
@@ -149,7 +148,7 @@
     barrier = pltpu.get_barrier_semaphore()
     for device in place.neighbours():
         pl.semaphore_signal(barrier, inc=1, device_id={"ctx": device}, device_id_type=MESH)
-    pl.semaphore_wait(barrier, 5)
+    pl.semaphore_wait(barrier, 7)
     in_turn(
         gather_stream(place, True, k_ref, gk_ref, own_sem.at[0], k_send, k_recv),
         gather_stream(place, False, v_ref, gv_ref, own_sem.at[1], v_send, v_recv),
@@ -164,7 +163,7 @@
 
 
 def scatter_stream(place, fast_is_x, term, out, bufs, send_sem, recv_sem):
-    outgoing, sib, acc, across, from_low, from_high, line, near_a, near_b, end_low, end_high = bufs
+    outgoing, sib, acc, across, from_low, from_high, line, far, end_low, end_high = bufs
     fast, slow, along_fast, along_slow = place.order(fast_is_x)
     sent, send = sender(send_sem, recv_sem)
     order = (2, 1, -1, 0)
@@ -228,32 +227,23 @@
         line[slot(n)] = add(acc[block(0, n)], from_low[slot(n)], from_high[slot(n)])
 
     settle(0)
-    send(16, line.at[pl.ds(0, 1)], near_a, along_fast(1))
-    send(17, line.at[pl.ds(1, 1)], near_b, along_fast(-1))
+    send(16, line.at[slot(0)], far, along_fast(2))
     yield
     settle(1)
-    send(18, line.at[pl.ds(3, 1)], end_low.at[pl.ds(1, 1)], along_fast(1))
+    send(17, line.at[slot(1)], end_low, along_fast(1))
     yield
     settle(2)
-    send(19, line.at[pl.ds(4, 1)], end_high.at[pl.ds(0, 1)], along_fast(-1))
-    yield
-    sent[16].wait_recv()
-    line[pl.ds(2, 1)] = add(line[pl.ds(2, 1)], near_a[...])
-    send(20, line.at[pl.ds(2, 1)], end_low.at[pl.ds(0, 1)], along_fast(1))
-    yield
-    sent[17].wait_recv()
-    line[pl.ds(5, 1)] = add(line[pl.ds(5, 1)], near_b[...])
-    send(21, line.at[pl.ds(5, 1)], end_high.at[pl.ds(1, 1)], along_fast(-1))
+    send(18, line.at[slot(2)], end_high, along_fast(-1))
     yield
     settle(3)
-    for i in (18, 19, 20, 21):
+    for i in (16, 17, 18):
         sent[i].wait_recv()
-    out[...] = add(line[slot(3)], end_low[...], end_high[...])
-    for i in range(22):
-        sent[i].wait_send()
-
-
-SCATTER_BUFS = (SIDE * GROUP, SIDE * GROUP, SIDE * GROUP, GROUP, GROUP, GROUP, GROUP, 1, 1, 2, 2)
+    out[...] = add(line[slot(3)], end_low[...], end_high[...], far[...])
+    for copy in sent.values():
+        copy.wait_send()
+
+
+SCATTER_BUFS = (SIDE * GROUP, SIDE * GROUP, SIDE * GROUP, GROUP, GROUP, GROUP, GROUP, 2, 2, 2)
 
 
 def dot(a, b, over):
@@ -372,7 +362,7 @@
 
         return term
 
-    pl.semaphore_wait(barrier, 7)
+    pl.semaphore_wait(barrier, 9)
     hand = pltpu.make_async_remote_copy(
         src_ref=dq_ref, dst_ref=handed_ref, send_sem=hand_sem.at[0], recv_sem=hand_sem.at[1],
         device_id={"pipe": below}, device_id_type=MESH,
@@ -404,7 +394,8 @@
         in_specs=[vmem] * 2,
         out_specs=(vmem, vmem),
         scratch_shapes=[dma((2,))] + [dma((23,))] * 4,
-        compiler_params=pltpu.CompilerParams(collective_id=0, has_side_effects=True),
+        compiler_params=pltpu.CompilerParams(collective_id=0, has_side_effects=True, vmem_limit_bytes=8 << 20),
+        cost_estimate=pl.CostEstimate(flops=2**33, bytes_accessed=2**26, transcendentals=0),
         name="gather_keys_values",
     )(keys.reshape(2, ST, HD), values.reshape(2, ST, HD))
     bufs = [pltpu.VMEM((n, ST, HD), BF16) for n in SCATTER_BUFS]
@@ -426,9 +417,10 @@
         ]
         + bufs
         + bufs
-        + [dma((22,))] * 4
+        + [dma((19,))] * 4
         + [dma((2,))],
-        compiler_params=pltpu.CompilerParams(collective_id=1, has_side_effects=True),
+        compiler_params=pltpu.CompilerParams(collective_id=1, has_side_effects=True, vmem_limit_bytes=28 << 20),
+        cost_estimate=pl.CostEstimate(flops=2**33, bytes_accessed=2**26, transcendentals=0),
         name="attend_scatter",
     )(doc_lengths, pair_of_rank, queries[0], attn_out[0], grad_out[0], all_keys, all_values)
     query_grad, handed, key_grad, value_grad = pl.pallas_call(
@@ -436,6 +428,7 @@
         out_shape=(wide, wide, own, own),
         in_specs=[vmem] * 4,
         out_specs=(vmem,) * 4,
+        compiler_params=pltpu.CompilerParams(vmem_limit_bytes=4 << 20),
         name="finish",
     )(*results)
     return (

time: 54.8 us -> 47.6 us (0.87)
  Pallas kernels: 53.9 us -> 44.3 us
  local copies, waits for them, and re-layouts: 0 us -> 2.15 us
    pallas_call x1, Pallas kernels: 23.3 us -> 18 us  [on_device(): pl.pallas_call(gather_kernel, out_shape=(full, full), in_specs=[vmem] * 2...]
    pallas_call x1, Pallas kernels: 28.8 us -> 25.4 us  [on_device(): pl.pallas_call(attend_scatter_kernel, out_shape=(wide, wide, own, own), i...]
    unnamed x0 -> x14, local copies, waits for them, and re-layouts: none -> 2.15 us
    pallas_call x1, Pallas kernels: 1.85 us -> 0.84 us  [on_device(): pl.pallas_call(finish_kernel, out_shape=(wide, wide, own, own), in_specs=...]
where the time goes in v4:
time: 47.6 us; the launch traced here: 47.2 us
  Pallas kernels  44.3 us (93%)
  local copies, waits for them, and re-layouts  2.15 us (5%)
  between operations  0.7 us (1%)
    pallas_call x1, Pallas kernels, on_device(): pl.pallas_call(attend_scatter_kernel, out_shape=(wide, wide, own, own), i...  25.4 us
    pallas_call x1, Pallas kernels, on_device(): pl.pallas_call(gather_kernel, out_shape=(full, full), in_specs=[vmem] * 2...  18 us
    unnamed x14, local copies, waits for them, and re-layouts  2.15 us

profile of v4, /device:TPU:6, one launch (start us, length us, event | category | flops | bytes accessed | tf_op | source)
XLA Modules:
  0.0 47.2 jit_solution(9519080336260097638)
XLA Ops:
  0.6 0.0 copy-start.3
  0.6 0.7 %copy-done.3 = bf16[1,128,128]{2,1,0:T(8,128)(2,1)S(1)} copy-done((bf16[1,128,128]{2,1,0:T(8,128)(2,1)S(1)}, bf16[1,128,128]{2,1,0:T(8,128)(2,1)}, u32[]{:S(2)}) %copy-start.3) | copy-done | bytes 32792
  1.4 0.0 copy-start.4
  1.4 0.8 %copy-done.4 = bf16[1,128,128]{2,1,0:T(8,128)(2,1)S(1)} copy-done((bf16[1,128,128]{2,1,0:T(8,128)(2,1)S(1)}, bf16[1,128,128]{2,1,0:T(8,128)(2,1)}, u32[]{:S(2)}) %copy-start.4) | copy-done | bytes 32792
  2.1 0.0 copy-start
  2.2 0.0 copy-start.1
  2.2 0.0 copy-start.2
  2.2 18.0 %gather_keys_values.1 = (bf16[64,64,128]{2,1,0:T(8,128)(2,1)S(1)}, bf16[64,64,128]{2,1,0:T(8,128)(2,1)S(1)}) custom-call(bf16[2,64,128]{2,1,0:T(8,128)(2,1)S(1)} %bitcast.12, bf16[2,64,128]{2,1,0:T(8,128)(2,1)S(1)} %bitcast.13), custom_call_target="tpu_custom_call" | custom-call | flops 8589934592 | bytes 67108864 | tf_op jit(solution)/shard_map/gather_keys_values/pallas_call | solution.py:391
  20.2 0.0 copy-start.5
  20.2 0.0 copy-start.6
  20.2 0.0 copy-done
  20.2 0.0 copy-done.1
  20.2 0.0 copy-done.2
  20.3 0.6 %copy-done.5 = s32[16]{0:T(128)S(1)} copy-done((s32[16]{0:T(128)S(1)}, s32[16]{0:T(128)}, u32[]{:S(2)}) %copy-start.5) | copy-done | bytes 88
  20.9 0.0 copy-done.6
  20.9 25.4 %attend_scatter.1 = (bf16[128,1024]{1,0:T(8,128)(2,1)S(1)}, bf16[128,1024]{1,0:T(8,128)(2,1)S(1)}, bf16[2,64,128]{2,1,0:T(8,128)(2,1)S(1)}, bf16[2,64,128]{2,1,0:T(8,128)(2,1)S(1)}) custom-call(s32[16]{0:T(128)S(1)} %copy-done.5, s32[32]{0:T(128)S(1)} %copy-done.6, bf16[128,1024]{1,0:T(8,128)(2,1)S(1)} %bitcast.9, bf16[128,1024]{1,0:T(8,128)(2,1)S(1)} %bitcast.10, ...), custom_call_target="tpu_custom_call" | custom-call | flops 8589934592 | bytes 67108864 | tf_op jit(solution)/shard_map/attend_scatter/pallas_call | solution.py:403
  46.3 0.8 %finish.1 = (bf16[128,1024]{1,0:T(8,128)(2,1)}, bf16[128,1024]{1,0:T(8,128)(2,1)}, bf16[2,64,128]{2,1,0:T(8,128)(2,1)}, bf16[2,64,128]{2,1,0:T(8,128)(2,1)}) custom-call(bf16[128,1024]{1,0:T(8,128)(2,1)S(1)} %get-tuple-element.16.refs_0_, bf16[128,1024]{1,0:T(8,128)(2,1)S(1)} %get-tuple-element.17.refs_1_, ...), custom_call_target="tpu_custom_call" | custom-call | tf_op jit(solution)/shard_map/finish/pallas_call | solution.py:426
Async XLA Ops:
  0.6 0.8 %copy-start.3 = (bf16[1,128,128]{2,1,0:T(8,128)(2,1)S(1)}, bf16[1,128,128]{2,1,0:T(8,128)(2,1)}, u32[]{:S(2)}) copy-start(bf16[1,128,128]{2,1,0:T(8,128)(2,1)} %param.8) | copy-start | bytes 98308
  1.4 0.8 %copy-start.4 = (bf16[1,128,128]{2,1,0:T(8,128)(2,1)S(1)}, bf16[1,128,128]{2,1,0:T(8,128)(2,1)}, u32[]{:S(2)}) copy-start(bf16[1,128,128]{2,1,0:T(8,128)(2,1)} %param.9) | copy-start | bytes 98308
  2.1 18.1 %copy-start = (bf16[1,128,1024]{2,1,0:T(8,128)(2,1)S(1)}, bf16[1,128,1024]{2,1,0:T(8,128)(2,1)}, u32[]{:S(2)}) copy-start(bf16[1,128,1024]{2,1,0:T(8,128)(2,1)} %param.7) | copy-start | bytes 786436
  2.2 18.1 %copy-start.1 = (bf16[1,128,1024]{2,1,0:T(8,128)(2,1)S(1)}, bf16[1,128,1024]{2,1,0:T(8,128)(2,1)}, u32[]{:S(2)}) copy-start(bf16[1,128,1024]{2,1,0:T(8,128)(2,1)} %param.10) | copy-start | bytes 786436
  2.2 18.1 %copy-start.2 = (bf16[1,128,1024]{2,1,0:T(8,128)(2,1)S(1)}, bf16[1,128,1024]{2,1,0:T(8,128)(2,1)}, u32[]{:S(2)}) copy-start(bf16[1,128,1024]{2,1,0:T(8,128)(2,1)} %param.11) | copy-start | bytes 786436
  20.2 0.7 %copy-start.5 = (s32[16]{0:T(128)S(1)}, s32[16]{0:T(128)}, u32[]{:S(2)}) copy-start(s32[16]{0:T(128)} %docs.1) | copy-start | bytes 196
  20.2 0.7 %copy-start.6 = (s32[32]{0:T(128)S(1)}, s32[32]{0:T(128)}, u32[]{:S(2)}) copy-start(s32[32]{0:T(128)} %pairs.1) | copy-start | bytes 388

commit v5 on v4

--- a/solution.py
+++ b/solution.py
@@ -183,33 +183,38 @@
         y, x = (line_at, n // 2) if fast_is_x else (n // 2, line_at)
         return term((y * SIDE + x) * 2 + core, half)
 
-    def fill(d):
-        for n in range(GROUP):
-            outgoing[step(slow, d) * GROUP + n] = own_term(1 - place.core, d, n)
+    def own_terms(core, d):
+        return jnp.stack([own_term(core, d, n) for n in range(GROUP)])
+
+    def prepare(d):
+        acc[at(d)] = own_terms(place.core, d)
 
     def merge(d):
-        for n in range(GROUP):
-            index = step(slow, d) * GROUP + n
-            acc[index] = add(own_term(place.core, d, n), sib[index])
+        acc[at(d)] = add(acc[at(d)], sib[at(d)])
 
     for i, d in enumerate((2, 1, -1, 0)):
-        fill(d)
+        outgoing[at(d)] = own_terms(1 - place.core, d)
         send(i, outgoing.at[at(d)], sib.at[at(d)], place.sibling())
         yield
+    prepare(2)
+    yield
     sent[0].wait_recv()
     merge(2)
     for n in range(4):
         send(4 + n, acc.at[block(2, n)], across.at[slot(n)], along_slow(way[n]))
+    prepare(1)
     yield
     sent[1].wait_recv()
     merge(1)
     for n in (1, 2):
         send(8 + n, acc.at[block(1, n)], from_low.at[slot(n)], along_slow(1))
+    prepare(-1)
     yield
     sent[2].wait_recv()
     merge(-1)
     for n in (0, 3):
         send(8 + n, acc.at[block(-1, n)], from_high.at[slot(n)], along_slow(-1))
+    prepare(0)
     yield
     sent[3].wait_recv()
     merge(0)
@@ -380,6 +385,10 @@
         target[...] = source[...]
 
 
+def in_hbm(x):
+    return pltpu.with_memory_space_constraint(x, pltpu.HBM)
+
+
 def on_device(queries, keys, values, attn_out, grad_out, doc_lengths, pair_of_rank):
     vmem = pl.BlockSpec(memory_space=pltpu.VMEM)
     smem = pl.BlockSpec(memory_space=pltpu.SMEM)
@@ -391,13 +400,13 @@
     all_keys, all_values = pl.pallas_call(
         gather_kernel,
         out_shape=(full, full),
-        in_specs=[vmem] * 2,
+        in_specs=[pl.BlockSpec(memory_space=pltpu.HBM)] * 2,
         out_specs=(vmem, vmem),
         scratch_shapes=[dma((2,))] + [dma((23,))] * 4,
         compiler_params=pltpu.CompilerParams(collective_id=0, has_side_effects=True, vmem_limit_bytes=8 << 20),
         cost_estimate=pl.CostEstimate(flops=2**33, bytes_accessed=2**26, transcendentals=0),
         name="gather_keys_values",
-    )(keys.reshape(2, ST, HD), values.reshape(2, ST, HD))
+    )(in_hbm(keys.reshape(2, ST, HD)), in_hbm(values.reshape(2, ST, HD)))
     bufs = [pltpu.VMEM((n, ST, HD), BF16) for n in SCATTER_BUFS]
     wide = jax.ShapeDtypeStruct((tok, HQ * HD), BF16)
     results = pl.pallas_call(
@@ -422,7 +431,7 @@
         compiler_params=pltpu.CompilerParams(collective_id=1, has_side_effects=True, vmem_limit_bytes=28 << 20),
         cost_estimate=pl.CostEstimate(flops=2**33, bytes_accessed=2**26, transcendentals=0),
         name="attend_scatter",
-    )(doc_lengths, pair_of_rank, queries[0], attn_out[0], grad_out[0], all_keys, all_values)
+    )(in_hbm(doc_lengths), in_hbm(pair_of_rank), queries[0], attn_out[0], grad_out[0], all_keys, all_values)
     query_grad, handed, key_grad, value_grad = pl.pallas_call(
         finish_kernel,
         out_shape=(wide, wide, own, own),

time: 47.6 us -> 45.5 us (0.956)
  local copies, waits for them, and re-layouts: 2.15 us -> 0.01 us
    unnamed x14 -> x6, local copies, waits for them, and re-layouts: 2.15 us -> 0.01 us
where the time goes in v5:
time: 45.5 us; the launch traced here: 45.2 us
  Pallas kernels  44.5 us (98%)
  between operations  0.7 us (2%)
    pallas_call x1, Pallas kernels, on_device(): pl.pallas_call(attend_scatter_kernel, out_shape=(wide, wide, own, own), i...  25.3 us
    pallas_call x1, Pallas kernels, on_device(): pl.pallas_call(gather_kernel, out_shape=(full, full), in_specs=[pl.BlockS...  18.3 us

profile of v5, /device:TPU:6, one launch (start us, length us, event | category | flops | bytes accessed | tf_op | source)
XLA Modules:
  0.0 45.2 jit_solution(9809364880465951479)
XLA Ops:
  0.6 0.0 copy-start
  0.6 0.0 copy-start.1
  0.7 0.0 copy-start.2
  0.7 18.3 %gather_keys_values.1 = (bf16[64,64,128]{2,1,0:T(8,128)(2,1)S(1)}, bf16[64,64,128]{2,1,0:T(8,128)(2,1)S(1)}) custom-call(bf16[2,64,128]{2,1,0:T(8,128)(2,1)} %bitcast.14, bf16[2,64,128]{2,1,0:T(8,128)(2,1)} %bitcast.15), custom_call_target="tpu_custom_call" | custom-call | flops 8589934592 | bytes 67108864 | tf_op jit(solution)/shard_map/gather_keys_values/pallas_call | solution.py:400
  19.0 0.0 copy-done
  19.0 0.0 copy-done.1
  19.0 0.0 copy-done.2
  19.0 25.3 %attend_scatter.1 = (bf16[128,1024]{1,0:T(8,128)(2,1)S(1)}, bf16[128,1024]{1,0:T(8,128)(2,1)S(1)}, bf16[2,64,128]{2,1,0:T(8,128)(2,1)S(1)}, bf16[2,64,128]{2,1,0:T(8,128)(2,1)S(1)}) custom-call(s32[16]{0:T(128)} %docs.1, s32[32]{0:T(128)} %pairs.1, bf16[128,1024]{1,0:T(8,128)(2,1)S(1)} %bitcast.9, bf16[128,1024]{1,0:T(8,128)(2,1)S(1)} %bitcast.10, ...), custom_call_target="tpu_custom_call" | custom-call | flops 8589934592 | bytes 67108864 | tf_op jit(solution)/shard_map/attend_scatter/pallas_call | solution.py:412
  44.3 0.8 %finish.1 = (bf16[128,1024]{1,0:T(8,128)(2,1)}, bf16[128,1024]{1,0:T(8,128)(2,1)}, bf16[2,64,128]{2,1,0:T(8,128)(2,1)}, bf16[2,64,128]{2,1,0:T(8,128)(2,1)}) custom-call(bf16[128,1024]{1,0:T(8,128)(2,1)S(1)} %get-tuple-element.16.refs_0_, bf16[128,1024]{1,0:T(8,128)(2,1)S(1)} %get-tuple-element.17.refs_1_, ...), custom_call_target="tpu_custom_call" | custom-call | tf_op jit(solution)/shard_map/finish/pallas_call | solution.py:435
Async XLA Ops:
  0.6 18.3 %copy-start = (bf16[1,128,1024]{2,1,0:T(8,128)(2,1)S(1)}, bf16[1,128,1024]{2,1,0:T(8,128)(2,1)}, u32[]{:S(2)}) copy-start(bf16[1,128,1024]{2,1,0:T(8,128)(2,1)} %param.7) | copy-start | bytes 786436
  0.6 18.3 %copy-start.1 = (bf16[1,128,1024]{2,1,0:T(8,128)(2,1)S(1)}, bf16[1,128,1024]{2,1,0:T(8,128)(2,1)}, u32[]{:S(2)}) copy-start(bf16[1,128,1024]{2,1,0:T(8,128)(2,1)} %param.10) | copy-start | bytes 786436
  0.7 18.3 %copy-start.2 = (bf16[1,128,1024]{2,1,0:T(8,128)(2,1)S(1)}, bf16[1,128,1024]{2,1,0:T(8,128)(2,1)}, u32[]{:S(2)}) copy-start(bf16[1,128,1024]{2,1,0:T(8,128)(2,1)} %param.11) | copy-start | bytes 786436

commit v6 on v5

--- a/solution.py
+++ b/solution.py
@@ -201,11 +201,12 @@
     sent[0].wait_recv()
     merge(2)
     for n in range(4):
-        send(4 + n, acc.at[block(2, n)], across.at[slot(n)], along_slow(way[n]))
+        send(4 + n, acc.at[block(2, n)], across.at[slot(n)], along_slow(way[n] if n else 2))
     prepare(1)
     yield
     sent[1].wait_recv()
     merge(1)
+    send(12, acc.at[block(1, 0)], from_low.at[slot(0)], along_slow(1))
     for n in (1, 2):
         send(8 + n, acc.at[block(1, n)], from_low.at[slot(n)], along_slow(1))
     prepare(-1)
@@ -219,19 +220,19 @@
     sent[3].wait_recv()
     merge(0)
     yield
-    for n in range(4):
+    def settle(n, *more):
+        sent[8 + n].wait_recv()
+        sent[12 + n].wait_recv()
+        line[slot(n)] = add(acc[block(0, n)], from_low[slot(n)], from_high[slot(n)], *more)
+
+    for n in range(1, 4):
         sent[4 + n].wait_recv()
         acc[block(way[n], n)] = add(acc[block(way[n], n)], across[slot(n)])
         target = from_low if way[n] == 1 else from_high
         send(12 + n, acc.at[block(way[n], n)], target.at[slot(n)], along_slow(way[n]))
         yield
-
-    def settle(n):
-        sent[8 + n].wait_recv()
-        sent[12 + n].wait_recv()
-        line[slot(n)] = add(acc[block(0, n)], from_low[slot(n)], from_high[slot(n)])
-
-    settle(0)
+    sent[4].wait_recv()
+    settle(0, across[slot(0)])
     send(16, line.at[slot(0)], far, along_fast(2))
     yield
     settle(1)

time: 45.5 us -> 45.5 us (level); the launches traced: 45.2 us -> 44.7 us
  Pallas kernels: 44.5 us -> 44 us
    pallas_call x1, Pallas kernels: 25.3 us -> 24.9 us  [on_device(): pl.pallas_call(attend_scatter_kernel, out_shape=(wide, wide, own, own), i...]
where the time goes in v6:
time: 45.5 us; the launch traced here: 44.7 us
  Pallas kernels  44 us (97%)
  between operations  0.7 us (2%)
    pallas_call x1, Pallas kernels, on_device(): pl.pallas_call(attend_scatter_kernel, out_shape=(wide, wide, own, own), i...  24.9 us
    pallas_call x1, Pallas kernels, on_device(): pl.pallas_call(gather_kernel, out_shape=(full, full), in_specs=[pl.BlockS...  18.3 us

profile of v6, /device:TPU:6, one launch (start us, length us, event | category | flops | bytes accessed | tf_op | source)
XLA Modules:
  0.0 44.7 jit_solution(15768517536054552529)
XLA Ops:
  0.6 0.0 copy-start
  0.6 0.0 copy-start.1
  0.7 0.0 copy-start.2
  0.7 18.3 %gather_keys_values.1 = (bf16[64,64,128]{2,1,0:T(8,128)(2,1)S(1)}, bf16[64,64,128]{2,1,0:T(8,128)(2,1)S(1)}) custom-call(bf16[2,64,128]{2,1,0:T(8,128)(2,1)} %bitcast.14, bf16[2,64,128]{2,1,0:T(8,128)(2,1)} %bitcast.15), custom_call_target="tpu_custom_call" | custom-call | flops 8589934592 | bytes 67108864 | tf_op jit(solution)/shard_map/gather_keys_values/pallas_call | solution.py:401
  19.0 0.0 copy-done
  19.0 0.0 copy-done.1
  19.0 0.0 copy-done.2
  19.0 24.9 %attend_scatter.1 = (bf16[128,1024]{1,0:T(8,128)(2,1)S(1)}, bf16[128,1024]{1,0:T(8,128)(2,1)S(1)}, bf16[2,64,128]{2,1,0:T(8,128)(2,1)S(1)}, bf16[2,64,128]{2,1,0:T(8,128)(2,1)S(1)}) custom-call(s32[16]{0:T(128)} %docs.1, s32[32]{0:T(128)} %pairs.1, bf16[128,1024]{1,0:T(8,128)(2,1)S(1)} %bitcast.9, bf16[128,1024]{1,0:T(8,128)(2,1)S(1)} %bitcast.10, ...), custom_call_target="tpu_custom_call" | custom-call | flops 8589934592 | bytes 67108864 | tf_op jit(solution)/shard_map/attend_scatter/pallas_call | solution.py:413
  43.9 0.8 %finish.1 = (bf16[128,1024]{1,0:T(8,128)(2,1)}, bf16[128,1024]{1,0:T(8,128)(2,1)}, bf16[2,64,128]{2,1,0:T(8,128)(2,1)}, bf16[2,64,128]{2,1,0:T(8,128)(2,1)}) custom-call(bf16[128,1024]{1,0:T(8,128)(2,1)S(1)} %get-tuple-element.16.refs_0_, bf16[128,1024]{1,0:T(8,128)(2,1)S(1)} %get-tuple-element.17.refs_1_, ...), custom_call_target="tpu_custom_call" | custom-call | tf_op jit(solution)/shard_map/finish/pallas_call | solution.py:436
Async XLA Ops:
  0.6 18.3 %copy-start = (bf16[1,128,1024]{2,1,0:T(8,128)(2,1)S(1)}, bf16[1,128,1024]{2,1,0:T(8,128)(2,1)}, u32[]{:S(2)}) copy-start(bf16[1,128,1024]{2,1,0:T(8,128)(2,1)} %param.7) | copy-start | bytes 786436
  0.6 18.3 %copy-start.1 = (bf16[1,128,1024]{2,1,0:T(8,128)(2,1)S(1)}, bf16[1,128,1024]{2,1,0:T(8,128)(2,1)}, u32[]{:S(2)}) copy-start(bf16[1,128,1024]{2,1,0:T(8,128)(2,1)} %param.10) | copy-start | bytes 786436
  0.7 18.3 %copy-start.2 = (bf16[1,128,1024]{2,1,0:T(8,128)(2,1)S(1)}, bf16[1,128,1024]{2,1,0:T(8,128)(2,1)}, u32[]{:S(2)}) copy-start(bf16[1,128,1024]{2,1,0:T(8,128)(2,1)} %param.11) | copy-start | bytes 786436
